TPU v7x, 32 devices: a whole 2x2x4 slice. The times are simulated.
32 devices in a mesh: grp: 2 (over x), probe: 8 (over z, y), beam: 2 (over core).
Axes of the slice: x: 2, y: 2, z: 4, core: 2. Of those that a mesh axis runs over, the one named last changes fastest.
Arguments:
- smatrix: bfloat16 [8192, 8, 512], P(('grp', 'beam'), 'probe'), parts along dimension 0, may hold values from -0.09375 to 0.09375
- aperture: float32 [4096], P('beam'), may hold values from 0.5 to 1.5
- aberration: float32 [4096], P('beam'), may hold values from -3.140625 to 3.140625
- beam_k: int32 [2, 4096], P(None, 'beam'), may hold values from -32 to 31, as said below
- probe_pos: int32 [2, 2048], P(None, 'probe'), may hold values from 0 to 1023
- patches: bfloat16 [128, 512], P(('grp', 'probe')), parts along dimension 0, may hold values from -6 to 6
- patch_col: int32 [128], P('grp'), parts along dimension 0, may hold values from 0 to 7, never falling along the last dimension, each value on 1 to 32 neighbouring positions
Outputs:
- ionization: float32 [16, 2048], P('grp', ('probe', 'beam')), parts along dimension 0
There are 2 independent parts, one for each index of `grp`. A program takes and returns all parts, laid end to end along the dimension named above; an argument that names none is the same for every part. Nothing has to cross between parts.
Inputs may be any that keep to these rules, and one draw needn't show every extreme that they name: `patch_col`: patches are ordered by atom column; each of the 8 columns has 1 to 32 patches, and some column has exactly 32. `beam_k`: no two beams have the same pair of indices.
All inputs are finite; a program needn't handle non-finite values.
Results may differ from a plain program's by a relative error of at most 0.005.
Values may be sent and summed in bfloat16 or wider, within the bound.
A program may use at most 128 MiB of HBM per device.

v0:
```python
import math

import jax
import jax.numpy as jnp
from jax import lax
from jax.sharding import PartitionSpec as P

PSIDE = 16
GRID = 1024


def coefficients(beam_k, aperture, aberration, positions):
    turn_count = jnp.mod(
        positions[0][:, None] * beam_k[0][None, :] + positions[1][:, None] * beam_k[1][None, :],
        GRID,
    )
    phase_angle = aberration[None, :] + 2.0 * math.pi / GRID * turn_count.astype(jnp.float32)
    real_coef = (aperture[None, :] * jnp.cos(phase_angle)).astype(jnp.bfloat16)
    imag_coef = (-(aperture[None, :] * jnp.sin(phase_angle))).astype(jnp.bfloat16)
    return (real_coef, imag_coef)


def detector(edge_count):
    half_side = edge_count // 2
    pixel_index = jnp.arange(edge_count * edge_count, dtype=jnp.int32)
    mode_index = jnp.arange(edge_count * half_side, dtype=jnp.int32)
    row_off = pixel_index // edge_count
    col_off = pixel_index % edge_count
    freq_first = mode_index // half_side - half_side
    freq_second = mode_index % half_side - edge_count // 4
    turn_count = jnp.mod(
        row_off[:, None] * freq_first[None, :] + col_off[:, None] * freq_second[None, :], edge_count
    )
    angle_value = 2.0 * math.pi / edge_count * turn_count.astype(jnp.float32)
    real_part = jnp.cos(angle_value)
    imag_part = -jnp.sin(angle_value)
    upper_rows = jnp.concatenate([real_part, imag_part], axis=1)
    lower_rows = jnp.concatenate([-imag_part, real_part], axis=1)
    return jnp.concatenate([upper_rows, lower_rows], axis=0).astype(jnp.bfloat16)


def patch_energy(picked, pot_rows, det_table):
    half_width = pot_rows.shape[-1] // 2
    psi_re = picked[..., :half_width].astype(jnp.float32)
    psi_im = picked[..., half_width:].astype(jnp.float32)
    pot_re = pot_rows[:, :half_width].astype(jnp.float32)
    pot_im = pot_rows[:, half_width:].astype(jnp.float32)
    wave_out = jnp.concatenate(
        [psi_re * pot_re - psi_im * pot_im, psi_re * pot_im + psi_im * pot_re], axis=-1
    ).astype(jnp.bfloat16)
    projected = jnp.einsum("rjx,xq->rjq", wave_out, det_table, preferred_element_type=jnp.float32)
    return jnp.sum(projected * projected, axis=-1) / float(half_width * (det_table.shape[1] // 2))


def combine(beam_terms):
    half_width = beam_terms.shape[-1] // 2
    return jnp.concatenate(
        [
            beam_terms[0, ..., :half_width] - beam_terms[1, ..., half_width:],
            beam_terms[0, ..., half_width:] + beam_terms[1, ..., :half_width],
        ],
        axis=-1,
    )


def spread_patches(psi, all_patches, patch_col, det_table):
    patch_total = all_patches.shape[0]
    group_size = math.gcd(patch_total, 16)
    column_count = psi.shape[1]
    col_groups = patch_col.reshape(patch_total // group_size, group_size)
    pot_groups = all_patches.reshape(patch_total // group_size, group_size, all_patches.shape[1])
    col_range = jnp.arange(column_count, dtype=jnp.int32)

    def add_block(running, blk_pair):
        col_ids, pot_rows = blk_pair
        picked = jnp.take(psi, col_ids, axis=1)
        energy = patch_energy(picked, pot_rows, det_table)
        onehot = (col_ids[:, None] == col_range[None, :]).astype(jnp.float32)
        return (
            running + jnp.einsum("rj,jc->cr", energy, onehot, precision=lax.Precision.HIGHEST),
            None,
        )

    running, _ = lax.scan(
        add_block, jnp.zeros((column_count, psi.shape[0]), jnp.float32), (col_groups, pot_groups)
    )
    return running


def apply_patches(psi_own, all_patches, patch_col, det_table):
    traded = lax.all_to_all(psi_own, "probe", split_axis=0, concat_axis=2, tiled=True)
    return spread_patches(traded[0], all_patches, patch_col, det_table)


def shards(smatrix, aperture, aberration, beam_k, probe_pos, patches, patch_col):
    probe_count = lax.axis_size("probe")
    beam_count = lax.axis_size("beam")
    all_patches = lax.all_gather(patches, "probe", axis=0, tiled=True)
    det_table = detector(PSIDE)
    col_dev = smatrix.shape[1]
    width_two = smatrix.shape[2]
    full_matrix, full_aperture, full_aberration, full_k = (
        lax.all_gather(smatrix, "beam", axis=0, tiled=True),
        lax.all_gather(aperture.astype(jnp.bfloat16), "beam", axis=0, tiled=True).astype(
            aperture.dtype
        ),
        lax.all_gather(aberration.astype(jnp.bfloat16), "beam", axis=0, tiled=True).astype(
            aberration.dtype
        ),
        lax.all_gather(beam_k, "beam", axis=1, tiled=True),
    )
    all_pos = lax.all_gather(probe_pos, "probe", axis=1, tiled=True)
    probe_total = all_pos.shape[1]
    half_probes = probe_total // (beam_count * probe_count)
    split_pos = all_pos.reshape(2, probe_count, beam_count, half_probes)
    mine = lax.dynamic_slice_in_dim(split_pos, lax.axis_index("beam"), 1, 2).reshape(
        2, probe_count * half_probes
    )
    row_total = probe_count * half_probes
    block_rows = math.gcd(row_total, 512)
    pos_blocks = mine.reshape(2, row_total // block_rows, block_rows).transpose(1, 0, 2)

    def whole_block(positions):
        real_coef, imag_coef = coefficients(full_k, full_aperture, full_aberration, positions)
        beam_terms = jnp.einsum(
            "kpb,bcx->kpcx",
            jnp.stack([real_coef, imag_coef]),
            full_matrix,
            preferred_element_type=jnp.float32,
        )
        return combine(beam_terms).astype(jnp.bfloat16)

    psi_own = lax.map(whole_block, pos_blocks).reshape(probe_count, half_probes, col_dev, width_two)
    return apply_patches(psi_own, all_patches, patch_col, det_table)


def solution(mesh):
    placed = (
        P(("grp", "beam"), "probe", None),
        P("beam"),
        P("beam"),
        P(None, "beam"),
        P(None, "probe"),
        P(("grp", "probe"), None),
        P("grp"),
    )
    return jax.shard_map(
        shards, mesh=mesh, in_specs=placed, out_specs=P("grp", ("probe", "beam")), check_vma=False
    )
```

profile of v0, /device:TPU:0, one launch (start us, length us, event | category | flops | bytes accessed | tf_op | source)
XLA Modules:
  0.0 199.8 jit_solution(7711247507291517825)
XLA Ops:
  6.6 4.0 %copy.15 = bf16[2048,1,512]{0,2,1:T(8,128)(2,1)} copy(bf16[2048,1,512]{2,0,1:T(8,128)(2,1)} %param.11) | data formatting | bytes 4194304 | tf_op args[0]
  10.6 2.0 all_gather.18
  12.6 1.8 all_gather.19
  14.4 27.8 %all_gather.20 = s32[2,2048]{1,0:T(2,128)S(1)} all-gather(s32[2,256]{1,0:T(2,128)S(1)} %copy-done.5), channel_id=1, replica_groups=mesh['grp'=2,'probe'=8,'beam'=2] {'probe'}, dimensions={1}, use_global_device_ids=true | all-gather | bytes 18432 | tf_op jit(solution)/shard_map/all_gather | solution.py:112
  42.3 1.8 all_gather.21
  44.2 82.0 %while.23 = (s32[]{:T(128)}, bf16[2,512,1,512]{3,1,0,2:T(8,128)(2,1)}, f32[4096]{0:T(1024)S(1)}, f32[4096]{0:T(1024)S(1)}, s32[2,2,512]{2,0,1:T(2,128)S(1)}, /*i...) while((s32[]{:T(128)}, bf16[2,512,1,512]{3,1,0,2:T(8,128)(2,1)}, ...), condition=%wide.region_1.2_spmd, body=%wide.region_0.1_spmd.sunk | while | flops 4346871808 | bytes 45756576 | solution.py:133
  44.3 35.1 %multiply_convert_fusion.2 = (bf16[1,512,4096]{2,1,0:T(8,128)(2,1)S(1)}, bf16[1,512,4096]{2,1,0:T(8,128)(2,1)S(1)}) fusion(s32[4096]{0:T(1024)S(1)} %bitcast.69, s32[512]{0:T(512)S(1)} %bitcast.72, s32[4096]{0:T(1024)S(1)} %bitcast.68, s32[512]{0:T(512)S(1)} %bitcast.71, f32[4096]{0:T(1024)S(1)} %get-tuple-element.349, f32[4096]{0:T(1024)S(1)} %get-tuple-element.348), kind=kLoop, calls=%fused_computation.14.clone.1 | loop fusion | flops 46137344 | bytes 8458240 | tf_op jit(solution)/shard_map/while/body/eval_jaxpr/convert_element_type | solution.py:18
  79.4 4.5 %fusion.66 = f32[2,512,1,512]{1,3,0,2:T(8,128)S(1)} fusion(bf16[4096,1,512]{0,2,1:T(8,128)(2,1)S(1)} %copy-done.7, bf16[1,512,4096]{2,1,0:T(8,128)(2,1)S(1)} %get-tuple-element.310, bf16[1,512,4096]{2,1,0:T(8,128)(2,1)S(1)} %get-tuple-element.311), kind=kOutput, calls=%fused_computation.16.clone.1 | convolution fusion | flops 4299161600 | bytes 14680064 | tf_op jit(solution)/shard_map/while/body/eval_jaxpr/kpb,bcx->kpcx/dot_general | solution.py:125
  84.4 0.8 constant_dynamic-update-slice_fusion.2
  85.3 35.1 %multiply_convert_fusion.2 = (bf16[1,512,4096]{2,1,0:T(8,128)(2,1)S(1)}, bf16[1,512,4096]{2,1,0:T(8,128)(2,1)S(1)}) fusion(s32[4096]{0:T(1024)S(1)} %bitcast.69, s32[512]{0:T(512)S(1)} %bitcast.72, s32[4096]{0:T(1024)S(1)} %bitcast.68, s32[512]{0:T(512)S(1)} %bitcast.71, f32[4096]{0:T(1024)S(1)} %get-tuple-element.349, f32[4096]{0:T(1024)S(1)} %get-tuple-element.348), kind=kLoop, calls=%fused_computation.14.clone.1 | loop fusion | flops 46137344 | bytes 8458240 | tf_op jit(solution)/shard_map/while/body/eval_jaxpr/convert_element_type | solution.py:18
  120.4 4.5 %fusion.66 = f32[2,512,1,512]{1,3,0,2:T(8,128)S(1)} fusion(bf16[4096,1,512]{0,2,1:T(8,128)(2,1)S(1)} %copy-done.7, bf16[1,512,4096]{2,1,0:T(8,128)(2,1)S(1)} %get-tuple-element.310, bf16[1,512,4096]{2,1,0:T(8,128)(2,1)S(1)} %get-tuple-element.311), kind=kOutput, calls=%fused_computation.16.clone.1 | convolution fusion | flops 4299161600 | bytes 14680064 | tf_op jit(solution)/shard_map/while/body/eval_jaxpr/kpb,bcx->kpcx/dot_general | solution.py:125
  125.4 0.8 constant_dynamic-update-slice_fusion.2
  126.2 4.0 %all-to-all-start = ((bf16[8,128,1,512]{3,1,2,0:T(8,128)(2,1)}), bf16[8,128,1,512]{3,1,2,0:T(8,128)(2,1)S(1)}, u32[]{:S(2)}, u32[]{:S(2)}) async-start(bf16[8,128,1,512]{3,1,2,0:T(8,128)(2,1)} %bitcast.9), calls=%async_computation | async-start | bytes 2097152 | tf_op jit(solution)/shard_map/all_to_all | solution.py:91
  130.3 46.0 %all_gather.23 = bf16[64,512]{1,0:T(8,128)(2,1)S(1)} all-gather(bf16[8,512]{1,0:T(8,128)(2,1)S(1)} %copy-done.2), channel_id=1, replica_groups=mesh['grp'=2,'probe'=8,'beam'=2] {'probe'}, dimensions={0}, use_global_device_ids=true | all-gather | bytes 73728 | tf_op jit(solution)/shard_map/all_gather | solution.py:98
  177.0 15.3 %while.24 = (s32[]{:T(128)}, f32[8,128]{1,0:T(8,128)S(1)}, s32[4,16]{1,0:T(4,128)S(1)}, bf16[128,8,512]{2,0,1:T(8,128)(2,1)S(1)}, bf16[4,16,512]{2,1,0:T(8,128)(...) while((s32[]{:T(128)}, f32[8,128]{1,0:T(8,128)S(1)}, s32[4,16]{1,0:T(4,128)S(1)}, ...), condition=%wide.region_4.5_spmd.clone, body=%wide.region_2.4_spmd.clone.sunk | while | flops 548613504 | bytes 15086163 | solution.py:84
  177.8 1.3 fusion.73
  179.1 0.7 fusion.74
  179.8 0.8 multiply_reduce_fusion.2
  181.7 1.3 fusion.73
  183.6 0.8 multiply_reduce_fusion.2
  185.5 1.3 fusion.73
  187.5 0.8 multiply_reduce_fusion.2
  189.3 1.3 fusion.73
  191.3 0.8 multiply_reduce_fusion.2
  (77 shorter events, 8.5 us)
Async XLA Ops:
  6.5 4.1 %copy-start.3 = (f32[2048]{0:T(1024)S(1)}, f32[2048]{0:T(1024)}, u32[]{:S(2)}) copy-start(f32[2048]{0:T(1024)} %param.12) | copy-start | bytes 24580
  6.5 6.1 %copy-start.4 = (f32[2048]{0:T(1024)S(1)}, f32[2048]{0:T(1024)}, u32[]{:S(2)}) copy-start(f32[2048]{0:T(1024)} %param.13) | copy-start | bytes 24580
  6.5 7.9 %copy-start.5 = (s32[2,256]{1,0:T(2,128)S(1)}, s32[2,256]{1,0:T(2,128)}, u32[]{:S(2)}) copy-start(s32[2,256]{1,0:T(2,128)} %param.15) | copy-start | bytes 6148
  6.5 35.8 %copy-start.1 = (s32[2,2048]{1,0:T(2,128)S(1)}, s32[2,2048]{1,0:T(2,128)}, u32[]{:S(2)}) copy-start(s32[2,2048]{1,0:T(2,128)} %param.14) | copy-start | bytes 49156
  6.5 37.6 %all-gather.2.cloned.1.call-start = ((), (), s32[]{:S(2)}) async-start(), calls=%async_computation.1 | async-start | bytes 6291456 | tf_op jit(solution)/shard_map/all_gather | solution.py:103
  44.2 86.0 %copy-start.6 = (s32[64]{0:T(128)S(1)}, s32[64]{0:T(128)}, u32[]{:S(2)}) copy-start(s32[64]{0:T(128)} %param.17) | copy-start | bytes 772
  44.2 86.1 %copy-start.2 = (bf16[8,512]{1,0:T(8,128)(2,1)S(1)}, bf16[8,512]{1,0:T(8,128)(2,1)}, u32[]{:S(2)}) copy-start(bf16[8,512]{1,0:T(8,128)(2,1)} %param.16) | copy-start | bytes 24580
  44.3 35.1 %copy-start.7 = (bf16[4096,1,512]{0,2,1:T(8,128)(2,1)S(1)}, bf16[4096,1,512]{0,2,1:T(8,128)(2,1)}, u32[]{:S(2)}) copy-start(bf16[4096,1,512]{0,2,1:T(8,128)(2,1)} %get-tuple-element.352) | copy-start | bytes 12582916 | tf_op jit(solution)/shard_map/while
  85.3 35.1 %copy-start.7 = (bf16[4096,1,512]{0,2,1:T(8,128)(2,1)S(1)}, bf16[4096,1,512]{0,2,1:T(8,128)(2,1)}, u32[]{:S(2)}) copy-start(bf16[4096,1,512]{0,2,1:T(8,128)(2,1)} %get-tuple-element.352) | copy-start | bytes 12582916 | tf_op jit(solution)/shard_map/while
  126.2 50.8 %all-to-all-start = ((bf16[8,128,1,512]{3,1,2,0:T(8,128)(2,1)}), bf16[8,128,1,512]{3,1,2,0:T(8,128)(2,1)S(1)}, u32[]{:S(2)}, u32[]{:S(2)}) async-start(bf16[8,128,1,512]{3,1,2,0:T(8,128)(2,1)} %bitcast.9), calls=%async_computation | async-start | bytes 2097152 | tf_op jit(solution)/shard_map/all_to_all | solution.py:91
  192.3 0.7 copy-start
Sparse Core Ops, SparseCore 0:
  10.7 16.3 all-gather.1
where the time goes:
time: 200 us
  other arithmetic  79.6 us (40%)
  blocking collectives  79.5 us (40%)
  between operations  13.5 us (7%)
  matrix products  13.1 us (7%)
  local copies, waits for them, and re-layouts  9.73 us (5%)
  starting transfers between devices  4.03 us (2%)
    convert_element_type x2, other arithmetic, coefficients(): real_coef = (aperture[None, :] * jnp.cos(phase_angle)).astype(jnp.bfloat16)  70.2 us
    all_gather x1, blocking collectives, shards(): all_patches = lax.all_gather(patches, 'probe', axis=0, tiled=True)  46 us
    all_gather x1, blocking collectives, shards(): all_pos = lax.all_gather(probe_pos, 'probe', axis=1, tiled=True)  27.8 us
    dot_general x2, matrix products, whole_block(): jnp.einsum('kpb,bcx->kpcx', jnp.stack([real_coef, imag_coef]), full_matri...  9.05 us
    select_n x8, other arithmetic, add_block(): picked = jnp.take(psi, col_ids, axis=1)  5.19 us
    unnamed x15, local copies, waits for them, and re-layouts  4.67 us
  transfers between devices with their start and end apart: 2, of which 0 were waited for; matrix products, arithmetic and copies ran while one was open for 0% of the time, Pallas kernels for 0%

commit v1 on v0

--- a/solution.py
+++ b/solution.py
@@ -9,14 +9,25 @@
 GRID = 1024
 
 
-def coefficients(beam_k, aperture, aberration, positions):
-    turn_count = jnp.mod(
-        positions[0][:, None] * beam_k[0][None, :] + positions[1][:, None] * beam_k[1][None, :],
-        GRID,
+def coefficients(beam_k, beam_cos, beam_sin, positions):
+    turn_count = (
+        positions[0][:, None] * beam_k[0][None, :] + positions[1][:, None] * beam_k[1][None, :]
+    ) & (GRID - 1)
+    quarter = GRID // 4
+    quadrant = lax.shift_right_arithmetic(turn_count + quarter // 2, quarter.bit_length() - 1)
+    resid = (turn_count - quadrant * quarter).astype(jnp.float32) * (2.0 * math.pi / GRID)
+    sq = resid * resid
+    sin_r = resid + resid * sq * (
+        -1.0 / 6 + sq * (1.0 / 120 + sq * (-1.0 / 5040 + sq * (1.0 / 362880)))
     )
-    phase_angle = aberration[None, :] + 2.0 * math.pi / GRID * turn_count.astype(jnp.float32)
-    real_coef = (aperture[None, :] * jnp.cos(phase_angle)).astype(jnp.bfloat16)
-    imag_coef = (-(aperture[None, :] * jnp.sin(phase_angle))).astype(jnp.bfloat16)
+    cos_r = 1.0 + sq * (-0.5 + sq * (1.0 / 24 + sq * (-1.0 / 720 + sq * (1.0 / 40320))))
+    odd = (quadrant & 1) == 1
+    cos_mag = jnp.where(odd, sin_r, cos_r)
+    sin_mag = jnp.where(odd, cos_r, sin_r)
+    cos_t = jnp.where(((quadrant + 1) & 2) != 0, -cos_mag, cos_mag)
+    sin_t = jnp.where((quadrant & 2) != 0, -sin_mag, sin_mag)
+    real_coef = (beam_cos[None, :] * cos_t - beam_sin[None, :] * sin_t).astype(jnp.bfloat16)
+    imag_coef = (-(beam_sin[None, :] * cos_t + beam_cos[None, :] * sin_t)).astype(jnp.bfloat16)
     return (real_coef, imag_coef)
 
 
@@ -99,16 +110,10 @@
     det_table = detector(PSIDE)
     col_dev = smatrix.shape[1]
     width_two = smatrix.shape[2]
-    full_matrix, full_aperture, full_aberration, full_k = (
-        lax.all_gather(smatrix, "beam", axis=0, tiled=True),
-        lax.all_gather(aperture.astype(jnp.bfloat16), "beam", axis=0, tiled=True).astype(
-            aperture.dtype
-        ),
-        lax.all_gather(aberration.astype(jnp.bfloat16), "beam", axis=0, tiled=True).astype(
-            aberration.dtype
-        ),
-        lax.all_gather(beam_k, "beam", axis=1, tiled=True),
-    )
+    full_matrix = lax.all_gather(smatrix, "beam", axis=0, tiled=True)
+    full_cos = lax.all_gather(aperture * jnp.cos(aberration), "beam", axis=0, tiled=True)
+    full_sin = lax.all_gather(aperture * jnp.sin(aberration), "beam", axis=0, tiled=True)
+    full_k = lax.all_gather(beam_k, "beam", axis=1, tiled=True)
     all_pos = lax.all_gather(probe_pos, "probe", axis=1, tiled=True)
     probe_total = all_pos.shape[1]
     half_probes = probe_total // (beam_count * probe_count)
@@ -121,7 +126,7 @@
     pos_blocks = mine.reshape(2, row_total // block_rows, block_rows).transpose(1, 0, 2)
 
     def whole_block(positions):
-        real_coef, imag_coef = coefficients(full_k, full_aperture, full_aberration, positions)
+        real_coef, imag_coef = coefficients(full_k, full_cos, full_sin, positions)
         beam_terms = jnp.einsum(
             "kpb,bcx->kpcx",
             jnp.stack([real_coef, imag_coef]),

time: 200 us -> 157 us (0.79)
  other arithmetic: 79.6 us -> 36.6 us
    convert_element_type x6 -> x2, other arithmetic: 70.3 us -> 27.3 us  [coefficients(): (beam_cos[None, :] * cos_t - beam_sin[None, :] * sin_t).astype(jnp.bfloat16)]
  transfers between devices with their start and end apart: 2 -> 2, of which waited for: 0 -> 0; matrix products, arithmetic and copies ran while one was open for 0% -> 1% of each run, Pallas kernels for 0% -> 0%
where the time goes in v1:
time: 157 us
  blocking collectives  79.5 us (51%)
  other arithmetic  36.6 us (23%)
  between operations  13.5 us (9%)
  matrix products  13.1 us (8%)
  local copies, waits for them, and re-layouts  9.69 us (6%)
  starting transfers between devices  4.03 us (3%)
    all_gather x1, blocking collectives, shards(): all_patches = lax.all_gather(patches, 'probe', axis=0, tiled=True)  46.1 us
    all_gather x1, blocking collectives, shards(): all_pos = lax.all_gather(probe_pos, 'probe', axis=1, tiled=True)  27.9 us
    convert_element_type x2, other arithmetic, coefficients(): (beam_cos[None, :] * cos_t - beam_sin[None, :] * sin_t).astype(jnp.bfloat16)  27.3 us
    dot_general x2, matrix products, whole_block(): jnp.einsum('kpb,bcx->kpcx', jnp.stack([real_coef, imag_coef]), full_matri...  9.05 us
    select_n x8, other arithmetic, add_block(): picked = jnp.take(psi, col_ids, axis=1)  5.19 us
    unnamed x15, local copies, waits for them, and re-layouts  4.64 us
    all_to_all x1, starting transfers between devices, apply_patches(): lax.all_to_all(psi_own, 'probe', split_axis=0, concat_axis=2, tiled=True)  4 us
    another operation x7, other arithmetic  3.76 us
  transfers between devices with their start and end apart: 2, of which 0 were waited for; matrix products, arithmetic and copies ran while one was open for 1% of the time, Pallas kernels for 0%

profile of v1, /device:TPU:0, one launch (start us, length us, event | category | flops | bytes accessed | tf_op | source)
XLA Modules:
  0.0 156.9 jit_solution(4632465547491041581)
XLA Ops:
  6.6 4.0 %copy.15 = bf16[2048,1,512]{0,2,1:T(8,128)(2,1)} copy(bf16[2048,1,512]{2,0,1:T(8,128)(2,1)} %param.11) | data formatting | bytes 4194304 | tf_op args[0]
  10.6 27.9 %all_gather.19 = s32[2,2048]{1,0:T(2,128)S(1)} all-gather(s32[2,256]{1,0:T(2,128)S(1)} %copy-done.5), channel_id=1, replica_groups=mesh['grp'=2,'probe'=8,'beam'=2] {'probe'}, dimensions={1}, use_global_device_ids=true | all-gather | bytes 18432 | tf_op jit(solution)/shard_map/all_gather | solution.py:117
  38.7 1.8 %all_gather.18 = f32[4096]{0:T(1024)S(1)} all-gather(f32[2048]{0:T(1024)S(1)} %get-tuple-element.159), channel_id=1, replica_groups=mesh['grp'=2,'probe'=8,'beam'=2] {'beam'}, dimensions={0}, use_global_device_ids=true | all-gather | bytes 24576 | tf_op jit(solution)/shard_map/all_gather | solution.py:114
  40.5 1.8 %all_gather.21 = f32[4096]{0:T(1024)S(1)} all-gather(f32[2048]{0:T(1024)S(1)} %get-tuple-element.158), channel_id=1, replica_groups=mesh['grp'=2,'probe'=8,'beam'=2] {'beam'}, dimensions={0}, use_global_device_ids=true | all-gather | bytes 24576 | tf_op jit(solution)/shard_map/all_gather | solution.py:115
  42.3 1.8 %all_gather.20 = s32[2,4096]{1,0:T(2,128)S(1)} all-gather(s32[2,2048]{1,0:T(2,128)S(1)} %copy-done.1), channel_id=1, replica_groups=mesh['grp'=2,'probe'=8,'beam'=2] {'beam'}, dimensions={1}, use_global_device_ids=true | all-gather | bytes 49152 | tf_op jit(solution)/shard_map/all_gather | solution.py:116
  44.2 39.0 %while.21 = (s32[]{:T(128)}, bf16[2,512,1,512]{3,1,0,2:T(8,128)(2,1)}, f32[4096]{0:T(1024)S(1)}, s32[2,2,512]{2,0,1:T(2,128)S(1)}, s32[2,4096]{1,0:T(2,128)S(1)}...) while((s32[]{:T(128)}, bf16[2,512,1,512]{3,1,0,2:T(8,128)(2,1)}, ...), condition=%wide.region_1.2_spmd, body=%wide.region_0.1_spmd.sunk | while | flops 4405592064 | bytes 45756576 | solution.py:138
  44.2 13.6 %subtract_convert_fusion.2 = (bf16[1,512,4096]{2,1,0:T(8,128)(2,1)S(1)}, bf16[1,512,4096]{2,1,0:T(8,128)(2,1)S(1)}) fusion(f32[4096]{0:T(1024)S(1)} %get-tuple-element.300, f32[4096]{0:T(1024)S(1)} %get-tuple-element.297, s32[4096]{0:T(1024)S(1)} %bitcast.69, s32[512]{0:T(512)S(1)} %bitcast.72, s32[4096]{0:T(1024)S(1)} %bitcast.68, s32[512]{0:T(512)S(1)} %bitcast.71), kind=kLoop, calls=%fused_computation.26.clone.1 | loop fusion | flops 104857600 | bytes 8458240 | tf_op jit(solution)/shard_map/while/body/eval_jaxpr/convert_element_type | solution.py:29
  57.9 4.5 %fusion.71 = f32[2,512,1,512]{1,3,0,2:T(8,128)S(1)} fusion(bf16[4096,1,512]{0,2,1:T(8,128)(2,1)S(1)} %copy-done.7, bf16[1,512,4096]{2,1,0:T(8,128)(2,1)S(1)} %get-tuple-element.259, bf16[1,512,4096]{2,1,0:T(8,128)(2,1)S(1)} %get-tuple-element.260), kind=kOutput, calls=%fused_computation.34.clone.1 | convolution fusion | flops 4299161600 | bytes 14680064 | tf_op jit(solution)/shard_map/while/body/eval_jaxpr/kpb,bcx->kpcx/dot_general | solution.py:130
  62.9 0.8 constant_dynamic-update-slice_fusion.2
  63.8 13.6 %subtract_convert_fusion.2 = (bf16[1,512,4096]{2,1,0:T(8,128)(2,1)S(1)}, bf16[1,512,4096]{2,1,0:T(8,128)(2,1)S(1)}) fusion(f32[4096]{0:T(1024)S(1)} %get-tuple-element.300, f32[4096]{0:T(1024)S(1)} %get-tuple-element.297, s32[4096]{0:T(1024)S(1)} %bitcast.69, s32[512]{0:T(512)S(1)} %bitcast.72, s32[4096]{0:T(1024)S(1)} %bitcast.68, s32[512]{0:T(512)S(1)} %bitcast.71), kind=kLoop, calls=%fused_computation.26.clone.1 | loop fusion | flops 104857600 | bytes 8458240 | tf_op jit(solution)/shard_map/while/body/eval_jaxpr/convert_element_type | solution.py:29
  77.4 4.5 %fusion.71 = f32[2,512,1,512]{1,3,0,2:T(8,128)S(1)} fusion(bf16[4096,1,512]{0,2,1:T(8,128)(2,1)S(1)} %copy-done.7, bf16[1,512,4096]{2,1,0:T(8,128)(2,1)S(1)} %get-tuple-element.259, bf16[1,512,4096]{2,1,0:T(8,128)(2,1)S(1)} %get-tuple-element.260), kind=kOutput, calls=%fused_computation.34.clone.1 | convolution fusion | flops 4299161600 | bytes 14680064 | tf_op jit(solution)/shard_map/while/body/eval_jaxpr/kpb,bcx->kpcx/dot_general | solution.py:130
  82.4 0.8 constant_dynamic-update-slice_fusion.2
  83.2 4.0 %all-to-all-start = ((bf16[8,128,1,512]{3,1,2,0:T(8,128)(2,1)}), bf16[8,128,1,512]{3,1,2,0:T(8,128)(2,1)S(1)}, u32[]{:S(2)}, u32[]{:S(2)}) async-start(bf16[8,128,1,512]{3,1,2,0:T(8,128)(2,1)} %bitcast.9), calls=%async_computation | async-start | bytes 2097152 | tf_op jit(solution)/shard_map/all_to_all | solution.py:102
  87.3 46.1 %all_gather.23 = bf16[64,512]{1,0:T(8,128)(2,1)S(1)} all-gather(bf16[8,512]{1,0:T(8,128)(2,1)S(1)} %copy-done.2), channel_id=1, replica_groups=mesh['grp'=2,'probe'=8,'beam'=2] {'probe'}, dimensions={0}, use_global_device_ids=true | all-gather | bytes 73728 | tf_op jit(solution)/shard_map/all_gather | solution.py:109
  134.1 15.3 %while.22 = (s32[]{:T(128)}, f32[8,128]{1,0:T(8,128)S(1)}, s32[4,16]{1,0:T(4,128)S(1)}, bf16[128,8,512]{2,0,1:T(8,128)(2,1)S(1)}, bf16[4,16,512]{2,1,0:T(8,128)(...) while((s32[]{:T(128)}, f32[8,128]{1,0:T(8,128)S(1)}, s32[4,16]{1,0:T(4,128)S(1)}, ...), condition=%wide.region_4.5_spmd.clone, body=%wide.region_2.4_spmd.clone.sunk | while | flops 548613504 | bytes 15086163 | solution.py:95
  134.9 1.3 fusion.78
  136.9 0.8 multiply_reduce_fusion.2
  138.7 1.3 fusion.78
  140.0 0.7 fusion.79
  140.7 0.8 multiply_reduce_fusion.2
  142.5 1.3 fusion.78
  144.5 0.8 multiply_reduce_fusion.2
  146.3 1.3 fusion.78
  148.3 0.8 multiply_reduce_fusion.2
  (74 shorter events, 8.6 us)
Async XLA Ops:
  6.5 4.1 %copy-start.5 = (s32[2,256]{1,0:T(2,128)S(1)}, s32[2,256]{1,0:T(2,128)}, u32[]{:S(2)}) copy-start(s32[2,256]{1,0:T(2,128)} %param.15) | copy-start | bytes 6148
  6.5 32.1 %copy-start.3 = (f32[2048]{0:T(1024)S(1)}, f32[2048]{0:T(1024)}, u32[]{:S(2)}) copy-start(f32[2048]{0:T(1024)} %param.12) | copy-start | bytes 24580
  6.5 32.1 %copy-start.4 = (f32[2048]{0:T(1024)S(1)}, f32[2048]{0:T(1024)}, u32[]{:S(2)}) copy-start(f32[2048]{0:T(1024)} %param.13) | copy-start | bytes 24580
  6.5 35.8 %copy-start.1 = (s32[2,2048]{1,0:T(2,128)S(1)}, s32[2,2048]{1,0:T(2,128)}, u32[]{:S(2)}) copy-start(s32[2,2048]{1,0:T(2,128)} %param.14) | copy-start | bytes 49156
  6.5 37.6 %all-gather.2.cloned.1.call-start = ((), (), s32[]{:S(2)}) async-start(), calls=%async_computation.1 | async-start | bytes 6291456 | tf_op jit(solution)/shard_map/all_gather | solution.py:113
  44.1 43.1 %copy-start.6 = (s32[64]{0:T(128)S(1)}, s32[64]{0:T(128)}, u32[]{:S(2)}) copy-start(s32[64]{0:T(128)} %param.17) | copy-start | bytes 772
  44.2 43.1 %copy-start.2 = (bf16[8,512]{1,0:T(8,128)(2,1)S(1)}, bf16[8,512]{1,0:T(8,128)(2,1)}, u32[]{:S(2)}) copy-start(bf16[8,512]{1,0:T(8,128)(2,1)} %param.16) | copy-start | bytes 24580
  44.2 13.7 %copy-start.7 = (bf16[4096,1,512]{0,2,1:T(8,128)(2,1)S(1)}, bf16[4096,1,512]{0,2,1:T(8,128)(2,1)}, u32[]{:S(2)}) copy-start(bf16[4096,1,512]{0,2,1:T(8,128)(2,1)} %get-tuple-element.301) | copy-start | bytes 12582916 | tf_op jit(solution)/shard_map/while
  63.7 13.7 %copy-start.7 = (bf16[4096,1,512]{0,2,1:T(8,128)(2,1)S(1)}, bf16[4096,1,512]{0,2,1:T(8,128)(2,1)}, u32[]{:S(2)}) copy-start(bf16[4096,1,512]{0,2,1:T(8,128)(2,1)} %get-tuple-element.301) | copy-start | bytes 12582916 | tf_op jit(solution)/shard_map/while
  83.2 50.9 %all-to-all-start = ((bf16[8,128,1,512]{3,1,2,0:T(8,128)(2,1)}), bf16[8,128,1,512]{3,1,2,0:T(8,128)(2,1)S(1)}, u32[]{:S(2)}, u32[]{:S(2)}) async-start(bf16[8,128,1,512]{3,1,2,0:T(8,128)(2,1)} %bitcast.9), calls=%async_computation | async-start | bytes 2097152 | tf_op jit(solution)/shard_map/all_to_all | solution.py:102
  149.4 0.7 copy-start
Sparse Core Ops, SparseCore 0:
  10.7 16.3 all-gather.1

commit v2 on v1

--- a/solution.py
+++ b/solution.py
@@ -115,27 +115,23 @@
     full_sin = lax.all_gather(aperture * jnp.sin(aberration), "beam", axis=0, tiled=True)
     full_k = lax.all_gather(beam_k, "beam", axis=1, tiled=True)
     all_pos = lax.all_gather(probe_pos, "probe", axis=1, tiled=True)
+    all_pos, all_patches = lax.optimization_barrier((all_pos, all_patches))
     probe_total = all_pos.shape[1]
     half_probes = probe_total // (beam_count * probe_count)
     split_pos = all_pos.reshape(2, probe_count, beam_count, half_probes)
     mine = lax.dynamic_slice_in_dim(split_pos, lax.axis_index("beam"), 1, 2).reshape(
         2, probe_count * half_probes
     )
-    row_total = probe_count * half_probes
-    block_rows = math.gcd(row_total, 512)
-    pos_blocks = mine.reshape(2, row_total // block_rows, block_rows).transpose(1, 0, 2)
-
-    def whole_block(positions):
-        real_coef, imag_coef = coefficients(full_k, full_cos, full_sin, positions)
-        beam_terms = jnp.einsum(
-            "kpb,bcx->kpcx",
-            jnp.stack([real_coef, imag_coef]),
-            full_matrix,
-            preferred_element_type=jnp.float32,
-        )
-        return combine(beam_terms).astype(jnp.bfloat16)
-
-    psi_own = lax.map(whole_block, pos_blocks).reshape(probe_count, half_probes, col_dev, width_two)
+    real_coef, imag_coef = coefficients(full_k, full_cos, full_sin, mine)
+    beam_terms = jnp.einsum(
+        "kpb,bcx->kpcx",
+        jnp.stack([real_coef, imag_coef]),
+        full_matrix,
+        preferred_element_type=jnp.float32,
+    )
+    psi_own = combine(beam_terms).astype(jnp.bfloat16).reshape(
+        probe_count, half_probes, col_dev, width_two
+    )
     return apply_patches(psi_own, all_patches, patch_col, det_table)
 
 

time: 157 us -> 169 us (1.076)
  waiting for transfers between devices: 0.02 us -> 26 us
  blocking collectives: 79.5 us -> 64.5 us
  local copies, waits for them, and re-layouts: 9.69 us -> 3.57 us
  matrix products: 13.1 us -> 17.2 us
  other arithmetic: 36.6 us -> 39.6 us
    all_to_all x1, waiting for transfers between devices: 0.01 us -> 25.3 us  [apply_patches(): lax.all_to_all(psi_own, 'probe', split_axis=0, concat_axis=2, tiled=True)]
    all_gather x1, blocking collectives: 46.1 us -> 32.6 us  [shards(): all_patches = lax.all_gather(patches, 'probe', axis=0, tiled=True)]
    dot_general x2 -> x1, matrix products: 9.05 us -> 13.2 us  [shards(): jnp.einsum('kpb,bcx->kpcx', jnp.stack([real_coef, imag_coef]), full_matri...]
    unnamed x15 -> x4, local copies, waits for them, and re-layouts: 4.64 us -> 0.66 us
    dynamic_update_slice x4 -> x0, local copies, waits for them, and re-layouts: 2.09 us -> none  [shards(): lax.map(whole_block, pos_blocks)]
    all_gather x1, blocking collectives: 27.9 us -> 26.2 us  [shards(): all_pos = lax.all_gather(probe_pos, 'probe', axis=1, tiled=True)]
    convert_element_type x2 -> x1, other arithmetic: 27.3 us -> 28.6 us  [coefficients(): (beam_cos[None, :] * cos_t - beam_sin[None, :] * sin_t).astype(jnp.bfloat16)]
    another operation x7 -> x6, other arithmetic: 3.76 us -> 3.72 us
  transfers between devices with their start and end apart: 2 -> 2, of which waited for: 0 -> 1; matrix products, arithmetic and copies ran while one was open for 1% -> 18% of each run, Pallas kernels for 0% -> 0%
where the time goes in v2:
time: 169 us; the launch traced here: 168 us
  blocking collectives  64.5 us (38%)
  other arithmetic  39.6 us (23%)
  waiting for transfers between devices  26 us (15%)
  matrix products  17.2 us (10%)
  between operations  13.5 us (8%)
  starting transfers between devices  3.86 us (2%)
  local copies, waits for them, and re-layouts  3.57 us (2%)
    all_gather x1, blocking collectives, shards(): all_patches = lax.all_gather(patches, 'probe', axis=0, tiled=True)  32.6 us
    convert_element_type x1, other arithmetic, coefficients(): (beam_cos[None, :] * cos_t - beam_sin[None, :] * sin_t).astype(jnp.bfloat16)  28.6 us
    all_gather x1, blocking collectives, shards(): all_pos = lax.all_gather(probe_pos, 'probe', axis=1, tiled=True)  26.2 us
    all_to_all x1, waiting for transfers between devices, apply_patches(): lax.all_to_all(psi_own, 'probe', split_axis=0, concat_axis=2, tiled=True)  25.3 us
    dot_general x1, matrix products, shards(): jnp.einsum('kpb,bcx->kpcx', jnp.stack([real_coef, imag_coef]), full_matri...  13.2 us
    select_n x8, other arithmetic, add_block(): picked = jnp.take(psi, col_ids, axis=1)  5.24 us
    all_to_all x1, starting transfers between devices, apply_patches(): lax.all_to_all(psi_own, 'probe', split_axis=0, concat_axis=2, tiled=True)  3.86 us
    another operation x6, other arithmetic  3.72 us
  transfers between devices with their start and end apart: 2, of which 1 were waited for; matrix products, arithmetic and copies ran while one was open for 18% of the time, Pallas kernels for 0%

profile of v2, /device:TPU:0, one launch (start us, length us, event | category | flops | bytes accessed | tf_op | source)
XLA Modules:
  0.0 168.4 jit_solution(5774982528233616721)
XLA Ops:
  6.5 0.7 all-gather.2.cloned.1.call-update
  7.3 32.6 %all_gather.20 = bf16[64,512]{1,0:T(8,128)(2,1)S(1)} all-gather(bf16[8,512]{1,0:T(8,128)(2,1)} %param.14), channel_id=1, replica_groups=mesh['grp'=2,'probe'=8,'beam'=2] {'probe'}, dimensions={0}, use_global_device_ids=true | all-gather | bytes 73728 | tf_op jit(solution)/shard_map/all_gather | solution.py:109
  39.8 26.2 %all_gather.19 = s32[2,2048]{1,0:T(2,128)S(1)} all-gather(s32[2,256]{1,0:T(2,128)} %param.13), channel_id=1, replica_groups=mesh['grp'=2,'probe'=8,'beam'=2] {'probe'}, dimensions={1}, use_global_device_ids=true | all-gather | bytes 18432 | tf_op jit(solution)/shard_map/all_gather | solution.py:117
  66.1 2.0 %all_gather.21 = s32[2,4096]{1,0:T(2,128)S(1)} all-gather(s32[2,2048]{1,0:T(2,128)} %param.12), channel_id=1, replica_groups=mesh['grp'=2,'probe'=8,'beam'=2] {'beam'}, dimensions={1}, use_global_device_ids=true | all-gather | bytes 49152 | tf_op jit(solution)/shard_map/all_gather | solution.py:116
  68.2 0.8 cosine_multiply_fusion
  68.9 1.8 %all_gather.18 = f32[4096]{0:T(1024)S(1)} all-gather(f32[2048]{0:T(1024)S(1)} %get-tuple-element.96), channel_id=1, replica_groups=mesh['grp'=2,'probe'=8,'beam'=2] {'beam'}, dimensions={0}, use_global_device_ids=true | all-gather | bytes 24576 | tf_op jit(solution)/shard_map/all_gather | solution.py:114
  70.8 1.8 %all_gather.22 = f32[4096]{0:T(1024)S(1)} all-gather(f32[2048]{0:T(1024)S(1)} %get-tuple-element.97), channel_id=1, replica_groups=mesh['grp'=2,'probe'=8,'beam'=2] {'beam'}, dimensions={0}, use_global_device_ids=true | all-gather | bytes 24576 | tf_op jit(solution)/shard_map/all_gather | solution.py:115
  72.6 28.6 %subtract_convert_fusion = (bf16[1,1024,4096]{2,1,0:T(8,128)(2,1)}, bf16[1,1024,4096]{2,1,0:T(8,128)(2,1)}) fusion(f32[4096]{0:T(1024)S(1)} %all_gather.22, f32[4096]{0:T(1024)S(1)} %all_gather.18, s32[4096]{0:T(1024)S(1)} %bitcast.53, s32[1024]{0:T(1024)S(1)} %bitcast.55, s32[4096]{0:T(1024)S(1)} %bitcast.52, s32[1024]{0:T(1024)S(1)} %bitcast.54), kind=kLoop, calls=%fused_computation.60 | loop fusion | flops 209715200 | bytes 16850944 | tf_op jit(solution)/shard_map/convert_element_type | solution.py:29
  101.2 13.2 %fusion.37 = f32[2,1024,1,512]{3,1,0,2:T(8,128)S(1)} fusion(bf16[4096,1,512]{2,0,1:T(8,128)(2,1)} %all-gather.2.cloned.1.call-done, bf16[1,1024,4096]{2,1,0:T(8,128)(2,1)} %get-tuple-element.91, bf16[1,1024,4096]{2,1,0:T(8,128)(2,1)} %get-tuple-element.90), kind=kOutput, calls=%fused_computation.68 | convolution fusion | flops 8598323200 | bytes 25165824 | tf_op jit(solution)/shard_map/kpb,bcx->kpcx/dot_general | solution.py:126
  114.7 1.1 pad_maximum_fusion
  115.7 3.9 %all-to-all-start = ((bf16[8,128,1,512]{3,1,2,0:T(8,128)(2,1)}), bf16[8,128,1,512]{3,1,2,0:T(8,128)(2,1)S(1)}, u32[]{:S(2)}, u32[]{:S(2)}) async-start(bf16[8,128,1,512]{3,1,2,0:T(8,128)(2,1)} %pad_maximum_fusion), calls=%async_computation | async-start | bytes 2097152 | tf_op jit(solution)/shard_map/all_to_all | solution.py:102
  120.4 25.3 %all-to-all-done = bf16[8,128,1,512]{3,1,2,0:T(8,128)(2,1)S(1)} async-done(((bf16[8,128,1,512]{3,1,2,0:T(8,128)(2,1)}), bf16[8,128,1,512]{3,1,2,0:T(8,128)(2,1)S(1)}, u32[]{:S(2)}, u32[]{:S(2)}) %all-to-all-start) | async-done | bytes 1048608 | tf_op jit(solution)/shard_map/all_to_all | solution.py:102
  145.7 15.3 %while.11 = (s32[]{:T(128)}, f32[8,128]{1,0:T(8,128)S(1)}, s32[4,16]{1,0:T(4,128)S(1)}, bf16[128,8,512]{2,0,1:T(8,128)(2,1)S(1)}, bf16[4,16,512]{2,1,0:T(8,128)(...) while((s32[]{:T(128)}, f32[8,128]{1,0:T(8,128)S(1)}, s32[4,16]{1,0:T(4,128)S(1)}, ...), condition=%wide.region_2.3_spmd.clone, body=%wide.region_0.2_spmd.clone.sunk | while | flops 548613504 | bytes 15086155 | solution.py:95
  146.4 1.3 fusion.68
  147.7 0.7 fusion.69
  148.4 0.8 multiply_reduce_fusion.2
  150.2 1.3 fusion.68
  151.6 0.7 fusion.69
  152.3 0.8 multiply_reduce_fusion.2
  154.1 1.3 fusion.68
  155.4 0.7 fusion.69
  156.1 0.8 multiply_reduce_fusion.2
  157.9 1.3 fusion.68
  159.9 0.8 multiply_reduce_fusion.2
  (45 shorter events, 6.4 us)
Async XLA Ops:
  6.5 94.7 %all-gather.2.cloned.1.call-start = ((), (), s32[]{:S(2)}) async-start(), calls=%async_computation.1 | async-start | bytes 6291456 | tf_op jit(solution)/shard_map/all_gather | solution.py:113
  114.4 5.2 %copy-start.1 = (s32[64]{0:T(128)S(1)}, s32[64]{0:T(128)}, u32[]{:S(2)}) copy-start(s32[64]{0:T(128)} %param.15) | copy-start | bytes 772
  115.7 30.0 %all-to-all-start = ((bf16[8,128,1,512]{3,1,2,0:T(8,128)(2,1)}), bf16[8,128,1,512]{3,1,2,0:T(8,128)(2,1)S(1)}, u32[]{:S(2)}, u32[]{:S(2)}) async-start(bf16[8,128,1,512]{3,1,2,0:T(8,128)(2,1)} %pad_maximum_fusion), calls=%async_computation | async-start | bytes 2097152 | tf_op jit(solution)/shard_map/all_to_all | solution.py:102
  160.9 0.7 copy-start
Sparse Core Ops, SparseCore 0:
  8.9 16.3 all-gather.1

commit v3 on v1

--- a/solution.py
+++ b/solution.py
@@ -106,15 +106,39 @@
 def shards(smatrix, aperture, aberration, beam_k, probe_pos, patches, patch_col):
     probe_count = lax.axis_size("probe")
     beam_count = lax.axis_size("beam")
-    all_patches = lax.all_gather(patches, "probe", axis=0, tiled=True)
+    probe_count_all = lax.axis_size("probe")
+    patch_size = patches.size
+    packed = jnp.concatenate(
+        [patches.astype(jnp.float32).reshape(-1), probe_pos.astype(jnp.float32).reshape(-1)]
+    )
+    gathered = lax.all_gather(packed, "probe", axis=0)
+    all_patches = (
+        gathered[:, :patch_size]
+        .reshape(probe_count_all * patches.shape[0], patches.shape[1])
+        .astype(patches.dtype)
+    )
+    all_pos = (
+        gathered[:, patch_size:]
+        .reshape(probe_count_all, 2, probe_pos.shape[1])
+        .transpose(1, 0, 2)
+        .reshape(2, probe_count_all * probe_pos.shape[1])
+        .astype(probe_pos.dtype)
+    )
     det_table = detector(PSIDE)
     col_dev = smatrix.shape[1]
     width_two = smatrix.shape[2]
     full_matrix = lax.all_gather(smatrix, "beam", axis=0, tiled=True)
-    full_cos = lax.all_gather(aperture * jnp.cos(aberration), "beam", axis=0, tiled=True)
-    full_sin = lax.all_gather(aperture * jnp.sin(aberration), "beam", axis=0, tiled=True)
-    full_k = lax.all_gather(beam_k, "beam", axis=1, tiled=True)
-    all_pos = lax.all_gather(probe_pos, "probe", axis=1, tiled=True)
+    beam_pack = jnp.stack(
+        [
+            aperture * jnp.cos(aberration),
+            aperture * jnp.sin(aberration),
+            beam_k[0].astype(jnp.float32),
+            beam_k[1].astype(jnp.float32),
+        ]
+    )
+    beam_all = lax.all_gather(beam_pack, "beam", axis=1, tiled=True)
+    full_cos, full_sin = beam_all[0], beam_all[1]
+    full_k = beam_all[2:].astype(beam_k.dtype)
     probe_total = all_pos.shape[1]
     half_probes = probe_total // (beam_count * probe_count)
     split_pos = all_pos.reshape(2, probe_count, beam_count, half_probes)

time: 157 us -> 139 us (0.89)
  blocking collectives: 79.5 us -> 34.2 us
  waiting for transfers between devices: 0.02 us -> 25.3 us
    all_gather x5 -> x2, blocking collectives: 79.5 us -> 34.2 us  [the longest x1 32.4 us: shards(): gathered = lax.all_gather(packed, 'probe', axis=0)]
    all_to_all x1, waiting for transfers between devices: 0.01 us -> 25.2 us  [apply_patches(): lax.all_to_all(psi_own, 'probe', split_axis=0, concat_axis=2, tiled=True)]
    another operation x7 -> x8, other arithmetic: 3.76 us -> 3.81 us
    unnamed x15 -> x19, local copies, waits for them, and re-layouts: 4.64 us -> 4.68 us
  transfers between devices with their start and end apart: 2 -> 2, of which waited for: 0 -> 1; matrix products, arithmetic and copies ran while one was open for 1% -> 1% of each run, Pallas kernels for 0% -> 0%
where the time goes in v3:
time: 139 us
  other arithmetic  36.6 us (26%)
  blocking collectives  34.2 us (25%)
  waiting for transfers between devices  25.3 us (18%)
  between operations  13.6 us (10%)
  matrix products  13.1 us (9%)
  local copies, waits for them, and re-layouts  9.82 us (7%)
  starting transfers between devices  5.52 us (4%)
    all_gather x1, blocking collectives, shards(): gathered = lax.all_gather(packed, 'probe', axis=0)  32.4 us
    convert_element_type x2, other arithmetic, coefficients(): (beam_cos[None, :] * cos_t - beam_sin[None, :] * sin_t).astype(jnp.bfloat16)  27.3 us
    all_to_all x1, waiting for transfers between devices, apply_patches(): lax.all_to_all(psi_own, 'probe', split_axis=0, concat_axis=2, tiled=True)  25.2 us
    dot_general x2, matrix products, whole_block(): jnp.einsum('kpb,bcx->kpcx', jnp.stack([real_coef, imag_coef]), full_matri...  9.06 us
    all_to_all x1, starting transfers between devices, apply_patches(): lax.all_to_all(psi_own, 'probe', split_axis=0, concat_axis=2, tiled=True)  5.48 us
    select_n x8, other arithmetic, add_block(): picked = jnp.take(psi, col_ids, axis=1)  5.24 us
    unnamed x19, local copies, waits for them, and re-layouts  4.68 us
    another operation x7, other arithmetic  3.77 us
  transfers between devices with their start and end apart: 2, of which 1 were waited for; matrix products, arithmetic and copies ran while one was open for 1% of the time, Pallas kernels for 0%

profile of v3, /device:TPU:0, one launch (start us, length us, event | category | flops | bytes accessed | tf_op | source)
XLA Modules:
  0.0 138.6 jit_solution(4428406749266956476)
XLA Ops:
  6.6 4.0 %copy.17 = bf16[2048,1,512]{0,2,1:T(8,128)(2,1)} copy(bf16[2048,1,512]{2,0,1:T(8,128)(2,1)} %param.11) | data formatting | bytes 4194304 | tf_op args[0]
  10.7 32.4 %all-gather.1 = f32[8,1,4608]{2,1,0:T(1,128)S(1)} all-gather(f32[1,1,4608]{2,1,0:T(1,128)S(1)} %reshape.635), channel_id=2, replica_groups=mesh['grp'=2,'probe'=8,'beam'=2] {'probe'}, dimensions={0}, use_global_device_ids=true | all-gather | bytes 165888 | tf_op jit(solution)/shard_map/all_gather | solution.py:114
  43.3 1.9 %all_gather.12 = f32[4,4096]{1,0:T(4,128)S(1)} all-gather(f32[4,2048]{1,0:T(4,128)S(1)} %pad_maximum_fusion.1), channel_id=1, replica_groups=mesh['grp'=2,'probe'=8,'beam'=2] {'beam'}, dimensions={1}, use_global_device_ids=true | all-gather | bytes 98304 | tf_op jit(solution)/shard_map/all_gather | solution.py:139
  45.2 39.0 %while.21 = (s32[]{:T(128)}, bf16[2,512,1,512]{3,1,0,2:T(8,128)(2,1)}, f32[1,4096]{1,0:T(1,128)S(1)}, s32[2,2,512]{2,0,1:T(2,128)S(1)}, s32[2,4096]{1,0:T(2,128)...) while((s32[]{:T(128)}, ...), condition=%wide.region_1.2_spmd, body=%wide.region_0.1_spmd.sunk | while | flops 4405592064 | bytes 45757076 | solution.py:162
  45.3 13.6 %subtract_convert_fusion.2 = (bf16[1,512,4096]{2,1,0:T(8,128)(2,1)S(1)}, bf16[1,512,4096]{2,1,0:T(8,128)(2,1)S(1)}) fusion(f32[4096]{0:T(1024)S(1)} %bitcast.90, f32[4096]{0:T(1024)S(1)} %bitcast.91, s32[4096]{0:T(1024)S(1)} %bitcast.89, s32[512]{0:T(512)S(1)} %bitcast.95, s32[4096]{0:T(1024)S(1)} %bitcast.88, s32[512]{0:T(512)S(1)} %bitcast.94), kind=kLoop, calls=%fused_computation.26.clone.1 | loop fusion | flops 104857600 | bytes 8458240 | tf_op jit(solution)/shard_map/while/body/eval_jaxpr/convert_element_type | solution.py:29
  59.0 4.5 %fusion.72 = f32[2,512,1,512]{1,3,0,2:T(8,128)S(1)} fusion(bf16[4096,1,512]{0,2,1:T(8,128)(2,1)S(1)} %copy-done.7, bf16[1,512,4096]{2,1,0:T(8,128)(2,1)S(1)} %get-tuple-element.270, bf16[1,512,4096]{2,1,0:T(8,128)(2,1)S(1)} %get-tuple-element.271), kind=kOutput, calls=%fused_computation.34.clone.1 | convolution fusion | flops 4299161600 | bytes 14680064 | tf_op jit(solution)/shard_map/while/body/eval_jaxpr/kpb,bcx->kpcx/dot_general | solution.py:154
  63.9 0.8 constant_dynamic-update-slice_fusion.2
  64.8 13.6 %subtract_convert_fusion.2 = (bf16[1,512,4096]{2,1,0:T(8,128)(2,1)S(1)}, bf16[1,512,4096]{2,1,0:T(8,128)(2,1)S(1)}) fusion(f32[4096]{0:T(1024)S(1)} %bitcast.90, f32[4096]{0:T(1024)S(1)} %bitcast.91, s32[4096]{0:T(1024)S(1)} %bitcast.89, s32[512]{0:T(512)S(1)} %bitcast.95, s32[4096]{0:T(1024)S(1)} %bitcast.88, s32[512]{0:T(512)S(1)} %bitcast.94), kind=kLoop, calls=%fused_computation.26.clone.1 | loop fusion | flops 104857600 | bytes 8458240 | tf_op jit(solution)/shard_map/while/body/eval_jaxpr/convert_element_type | solution.py:29
  78.5 4.5 %fusion.72 = f32[2,512,1,512]{1,3,0,2:T(8,128)S(1)} fusion(bf16[4096,1,512]{0,2,1:T(8,128)(2,1)S(1)} %copy-done.7, bf16[1,512,4096]{2,1,0:T(8,128)(2,1)S(1)} %get-tuple-element.270, bf16[1,512,4096]{2,1,0:T(8,128)(2,1)S(1)} %get-tuple-element.271), kind=kOutput, calls=%fused_computation.34.clone.1 | convolution fusion | flops 4299161600 | bytes 14680064 | tf_op jit(solution)/shard_map/while/body/eval_jaxpr/kpb,bcx->kpcx/dot_general | solution.py:154
  83.4 0.8 constant_dynamic-update-slice_fusion.2
  84.3 5.5 %all-to-all-start = ((bf16[8,128,1,512]{3,1,2,0:T(8,128)(2,1)}), bf16[8,128,1,512]{3,1,2,0:T(8,128)(2,1)S(1)}, u32[]{:S(2)}, u32[]{:S(2)}) async-start(bf16[8,128,1,512]{3,1,2,0:T(8,128)(2,1)} %bitcast.16), calls=%async_computation | async-start | bytes 2097152 | tf_op jit(solution)/shard_map/all_to_all | solution.py:102
  90.6 25.2 %all-to-all-done = bf16[8,128,1,512]{3,1,2,0:T(8,128)(2,1)S(1)} async-done(((bf16[8,128,1,512]{3,1,2,0:T(8,128)(2,1)}), bf16[8,128,1,512]{3,1,2,0:T(8,128)(2,1)S(1)}, u32[]{:S(2)}, u32[]{:S(2)}) %all-to-all-start) | async-done | bytes 1048608 | tf_op jit(solution)/shard_map/all_to_all | solution.py:102
  115.9 15.3 %while.22 = (s32[]{:T(128)}, f32[8,128]{1,0:T(8,128)S(1)}, s32[4,16]{1,0:T(4,128)S(1)}, bf16[128,8,512]{2,0,1:T(8,128)(2,1)S(1)}, bf16[4,16,512]{2,1,0:T(8,128)(...) while((s32[]{:T(128)}, f32[8,128]{1,0:T(8,128)S(1)}, s32[4,16]{1,0:T(4,128)S(1)}, ...), condition=%wide.region_4.5_spmd.clone, body=%wide.region_2.4_spmd.clone.sunk | while | flops 548613504 | bytes 15086155 | solution.py:95
  116.6 1.3 fusion.79
  117.9 0.7 fusion.80
  118.6 0.8 multiply_reduce_fusion.2
  120.4 1.3 fusion.79
  121.7 0.7 fusion.80
  122.4 0.8 multiply_reduce_fusion.2
  124.3 1.3 fusion.79
  126.3 0.8 multiply_reduce_fusion.2
  128.1 1.3 fusion.79
  129.4 0.7 fusion.80
  130.1 0.8 multiply_reduce_fusion.2
  (84 shorter events, 7.3 us)
Async XLA Ops:
  6.5 4.1 %copy-start.2 = (bf16[8,512]{1,0:T(8,128)(2,1)S(1)}, bf16[8,512]{1,0:T(8,128)(2,1)}, u32[]{:S(2)}) copy-start(bf16[8,512]{1,0:T(8,128)(2,1)} %param.16) | copy-start | bytes 24580
  6.5 4.1 %copy-start.5 = (s32[2,256]{1,0:T(2,128)S(1)}, s32[2,256]{1,0:T(2,128)}, u32[]{:S(2)}) copy-start(s32[2,256]{1,0:T(2,128)} %param.15) | copy-start | bytes 6148
  6.5 36.6 %copy-start.3 = (f32[2048]{0:T(1024)S(1)}, f32[2048]{0:T(1024)}, u32[]{:S(2)}) copy-start(f32[2048]{0:T(1024)} %param.12) | copy-start | bytes 24580
  6.5 36.6 %copy-start.4 = (f32[2048]{0:T(1024)S(1)}, f32[2048]{0:T(1024)}, u32[]{:S(2)}) copy-start(f32[2048]{0:T(1024)} %param.13) | copy-start | bytes 24580
  6.5 36.7 %copy-start.1 = (s32[2,2048]{1,0:T(2,128)S(1)}, s32[2,2048]{1,0:T(2,128)}, u32[]{:S(2)}) copy-start(s32[2,2048]{1,0:T(2,128)} %param.14) | copy-start | bytes 49156
  6.5 38.7 %all-gather.4.cloned.1.call-start = ((), (), s32[]{:S(2)}) async-start(), calls=%async_computation.1 | async-start | bytes 6291456 | tf_op jit(solution)/shard_map/all_gather | solution.py:130
  45.2 44.6 %copy-start.6 = (s32[64]{0:T(128)S(1)}, s32[64]{0:T(128)}, u32[]{:S(2)}) copy-start(s32[64]{0:T(128)} %param.17) | copy-start | bytes 772
  45.3 13.6 %copy-start.7 = (bf16[4096,1,512]{0,2,1:T(8,128)(2,1)S(1)}, bf16[4096,1,512]{0,2,1:T(8,128)(2,1)}, u32[]{:S(2)}) copy-start(bf16[4096,1,512]{0,2,1:T(8,128)(2,1)} %get-tuple-element.312) | copy-start | bytes 12582916 | tf_op jit(solution)/shard_map/while
  64.8 13.6 %copy-start.7 = (bf16[4096,1,512]{0,2,1:T(8,128)(2,1)S(1)}, bf16[4096,1,512]{0,2,1:T(8,128)(2,1)}, u32[]{:S(2)}) copy-start(bf16[4096,1,512]{0,2,1:T(8,128)(2,1)} %get-tuple-element.312) | copy-start | bytes 12582916 | tf_op jit(solution)/shard_map/while
  84.3 31.6 %all-to-all-start = ((bf16[8,128,1,512]{3,1,2,0:T(8,128)(2,1)}), bf16[8,128,1,512]{3,1,2,0:T(8,128)(2,1)S(1)}, u32[]{:S(2)}, u32[]{:S(2)}) async-start(bf16[8,128,1,512]{3,1,2,0:T(8,128)(2,1)} %bitcast.16), calls=%async_computation | async-start | bytes 2097152 | tf_op jit(solution)/shard_map/all_to_all | solution.py:102
  131.1 0.7 copy-start
Sparse Core Ops, SparseCore 0:
  10.7 16.3 all-gather.3

commit v4 on v3

--- a/solution.py
+++ b/solution.py
@@ -93,7 +93,10 @@
         )
 
     running, _ = lax.scan(
-        add_block, jnp.zeros((column_count, psi.shape[0]), jnp.float32), (col_groups, pot_groups)
+        add_block,
+        jnp.zeros((column_count, psi.shape[0]), jnp.float32),
+        (col_groups, pot_groups),
+        unroll=True,
     )
     return running
 

time: 139 us -> 146 us (1.050)
  local copies, waits for them, and re-layouts: 9.82 us -> 14.6 us
  other arithmetic: 36.6 us -> 38.4 us
    gather x4, local copies, waits for them, and re-layouts: 2.73 us -> 6.74 us  [add_block(): picked = jnp.take(psi, col_ids, axis=1)]
    select_n x8 -> x4, other arithmetic: 5.24 us -> 6.88 us  [add_block(): picked = jnp.take(psi, col_ids, axis=1)]
    unnamed x19 -> x21, local copies, waits for them, and re-layouts: 4.68 us -> 5.49 us
    another operation x7 -> x5, other arithmetic: 3.77 us -> 3.89 us
where the time goes in v4:
time: 146 us
  other arithmetic  38.4 us (26%)
  blocking collectives  34.2 us (23%)
  waiting for transfers between devices  25.2 us (17%)
  local copies, waits for them, and re-layouts  14.6 us (10%)
  matrix products  13.9 us (10%)
  between operations  13.7 us (9%)
  starting transfers between devices  5.63 us (4%)
    all_gather x1, blocking collectives, shards(): gathered = lax.all_gather(packed, 'probe', axis=0)  32.4 us
    convert_element_type x2, other arithmetic, coefficients(): (beam_cos[None, :] * cos_t - beam_sin[None, :] * sin_t).astype(jnp.bfloat16)  27.3 us
    all_to_all x1, waiting for transfers between devices, apply_patches(): lax.all_to_all(psi_own, 'probe', split_axis=0, concat_axis=2, tiled=True)  25.1 us
    dot_general x2, matrix products, whole_block(): jnp.einsum('kpb,bcx->kpcx', jnp.stack([real_coef, imag_coef]), full_matri...  9.05 us
    select_n x4, other arithmetic, add_block(): picked = jnp.take(psi, col_ids, axis=1)  6.88 us
    gather x4, local copies, waits for them, and re-layouts, add_block(): picked = jnp.take(psi, col_ids, axis=1)  6.74 us
    all_to_all x1, starting transfers between devices, apply_patches(): lax.all_to_all(psi_own, 'probe', split_axis=0, concat_axis=2, tiled=True)  5.62 us
    unnamed x21, local copies, waits for them, and re-layouts  5.49 us
  transfers between devices with their start and end apart: 2, of which 1 were waited for; matrix products, arithmetic and copies ran while one was open for 1% of the time, Pallas kernels for 0%

profile of v4, /device:TPU:0, one launch (start us, length us, event | category | flops | bytes accessed | tf_op | source)
XLA Modules:
  0.0 145.7 jit_solution(9574500198532155823)
XLA Ops:
  6.5 4.0 %copy.22 = bf16[2048,1,512]{0,2,1:T(8,128)(2,1)} copy(bf16[2048,1,512]{2,0,1:T(8,128)(2,1)} %param.11) | data formatting | bytes 4194304 | tf_op args[0]
  11.3 32.4 %all-gather.1 = f32[8,1,4608]{2,1,0:T(1,128)S(1)} all-gather(f32[1,1,4608]{2,1,0:T(1,128)S(1)} %reshape.657), channel_id=2, replica_groups=mesh['grp'=2,'probe'=8,'beam'=2] {'probe'}, dimensions={0}, use_global_device_ids=true | all-gather | bytes 165888 | tf_op jit(solution)/shard_map/all_gather | solution.py:117
  43.9 1.9 %all_gather.12 = f32[4,4096]{1,0:T(4,128)S(1)} all-gather(f32[4,2048]{1,0:T(4,128)S(1)} %pad_maximum_fusion.1), channel_id=1, replica_groups=mesh['grp'=2,'probe'=8,'beam'=2] {'beam'}, dimensions={1}, use_global_device_ids=true | all-gather | bytes 98304 | tf_op jit(solution)/shard_map/all_gather | solution.py:142
  45.8 39.0 %while.10 = (s32[]{:T(128)}, bf16[2,512,1,512]{3,1,0,2:T(8,128)(2,1)}, f32[1,4096]{1,0:T(1,128)S(1)}, s32[2,2,512]{2,0,1:T(2,128)S(1)}, s32[2,4096]{1,0:T(2,128)...) while((s32[]{:T(128)}, ...), condition=%wide.region_1.2_spmd, body=%wide.region_0.1_spmd.sunk | while | flops 4405592064 | bytes 45756576 | solution.py:165
  45.9 13.6 %subtract_convert_fusion.2 = (bf16[1,512,4096]{2,1,0:T(8,128)(2,1)S(1)}, bf16[1,512,4096]{2,1,0:T(8,128)(2,1)S(1)}) fusion(f32[4096]{0:T(1024)S(1)} %bitcast.83, f32[4096]{0:T(1024)S(1)} %bitcast.84, s32[4096]{0:T(1024)S(1)} %bitcast.82, s32[512]{0:T(512)S(1)} %bitcast.88, s32[4096]{0:T(1024)S(1)} %bitcast.81, s32[512]{0:T(512)S(1)} %bitcast.87), kind=kLoop, calls=%fused_computation.28.clone.1 | loop fusion | flops 104857600 | bytes 8458240 | tf_op jit(solution)/shard_map/while/body/eval_jaxpr/convert_element_type | solution.py:29
  59.5 4.5 %fusion.115 = f32[2,512,1,512]{1,3,0,2:T(8,128)S(1)} fusion(bf16[4096,1,512]{0,2,1:T(8,128)(2,1)S(1)} %copy-done.8, bf16[1,512,4096]{2,1,0:T(8,128)(2,1)S(1)} %get-tuple-element.200, bf16[1,512,4096]{2,1,0:T(8,128)(2,1)S(1)} %get-tuple-element.201), kind=kOutput, calls=%fused_computation.36.clone.1 | convolution fusion | flops 4299161600 | bytes 14680064 | tf_op jit(solution)/shard_map/while/body/eval_jaxpr/kpb,bcx->kpcx/dot_general | solution.py:157
  64.5 0.8 constant_dynamic-update-slice_fusion.2
  65.4 13.6 %subtract_convert_fusion.2 = (bf16[1,512,4096]{2,1,0:T(8,128)(2,1)S(1)}, bf16[1,512,4096]{2,1,0:T(8,128)(2,1)S(1)}) fusion(f32[4096]{0:T(1024)S(1)} %bitcast.83, f32[4096]{0:T(1024)S(1)} %bitcast.84, s32[4096]{0:T(1024)S(1)} %bitcast.82, s32[512]{0:T(512)S(1)} %bitcast.88, s32[4096]{0:T(1024)S(1)} %bitcast.81, s32[512]{0:T(512)S(1)} %bitcast.87), kind=kLoop, calls=%fused_computation.28.clone.1 | loop fusion | flops 104857600 | bytes 8458240 | tf_op jit(solution)/shard_map/while/body/eval_jaxpr/convert_element_type | solution.py:29
  79.1 4.5 %fusion.115 = f32[2,512,1,512]{1,3,0,2:T(8,128)S(1)} fusion(bf16[4096,1,512]{0,2,1:T(8,128)(2,1)S(1)} %copy-done.8, bf16[1,512,4096]{2,1,0:T(8,128)(2,1)S(1)} %get-tuple-element.200, bf16[1,512,4096]{2,1,0:T(8,128)(2,1)S(1)} %get-tuple-element.201), kind=kOutput, calls=%fused_computation.36.clone.1 | convolution fusion | flops 4299161600 | bytes 14680064 | tf_op jit(solution)/shard_map/while/body/eval_jaxpr/kpb,bcx->kpcx/dot_general | solution.py:157
  84.0 0.8 constant_dynamic-update-slice_fusion.2
  84.9 5.6 %all-to-all-start = ((bf16[8,128,1,512]{3,1,2,0:T(8,128)(2,1)}), bf16[8,128,1,512]{3,1,2,0:T(8,128)(2,1)S(1)}, u32[]{:S(2)}, u32[]{:S(2)}) async-start(bf16[8,128,1,512]{3,1,2,0:T(8,128)(2,1)} %bitcast.16), calls=%async_computation | async-start | bytes 2097152 | tf_op jit(solution)/shard_map/all_to_all | solution.py:105
  91.4 25.1 %all-to-all-done = bf16[8,128,1,512]{3,1,2,0:T(8,128)(2,1)S(1)} async-done(((bf16[8,128,1,512]{3,1,2,0:T(8,128)(2,1)}), bf16[8,128,1,512]{3,1,2,0:T(8,128)(2,1)S(1)}, u32[]{:S(2)}, u32[]{:S(2)}) %all-to-all-start) | async-done | bytes 1048608 | tf_op jit(solution)/shard_map/all_to_all | solution.py:105
  116.6 2.0 %gather_fusion = bf16[16,128,512]{2,1,0:T(8,128)(2,1)} fusion(bf16[128,8,512]{2,0,1:T(8,128)(2,1)S(1)} %bitcast.77, s32[1024]{0:T(1024)S(1)} %pad_clamp_fusion.3), kind=kCustom, calls=%fused_computation.clone | custom fusion | bytes 4194368 | tf_op jit(solution)/shard_map/eval_jaxpr/jit(_take)/gather | solution.py:87
  118.6 2.0 %gather_fusion.1 = bf16[16,128,512]{2,1,0:T(8,128)(2,1)} fusion(bf16[128,8,512]{2,0,1:T(8,128)(2,1)S(1)} %bitcast.78, s32[1024]{0:T(1024)S(1)} %pad_clamp_fusion.2), kind=kCustom, calls=%fused_computation.1.clone | custom fusion | bytes 4194368 | tf_op jit(solution)/shard_map/eval_jaxpr/jit(_take)/gather | solution.py:87
  120.6 2.0 %gather_fusion.2 = bf16[16,128,512]{2,1,0:T(8,128)(2,1)} fusion(bf16[128,8,512]{2,0,1:T(8,128)(2,1)S(1)} %bitcast.79, s32[1024]{0:T(1024)S(1)} %pad_clamp_fusion.1), kind=kCustom, calls=%fused_computation.2.clone | custom fusion | bytes 4194368 | tf_op jit(solution)/shard_map/eval_jaxpr/jit(_take)/gather | solution.py:87
  123.3 3.0 %fusion.57 = bf16[128,16,512]{2,1,0:T(8,128)(2,1)S(1)} fusion(bf16[16,128,512]{2,1,0:T(8,128)(2,1)} %gather_fusion, pred[16]{0:T(512)(128)(4,1)S(1)} %get-tuple-element.131), kind=kLoop, calls=%fused_computation.101 | loop fusion | flops 1048576 | bytes 4194320 | tf_op jit(solution)/shard_map/eval_jaxpr/jit(_take)/select_n | solution.py:87
  126.4 1.3 fusion.56
  127.6 1.5 fusion.23
  130.1 0.8 multiply_reduce_fusion.2
  131.0 0.8 copy-done
  131.8 1.3 fusion.55
  133.1 1.3 fusion.54
  134.3 1.5 %fusion.31 = (bf16[128,16,256]{2,1,0:T(8,128)(2,1)S(1)}, bf16[128,16,256]{2,1,0:T(8,128)(2,1)S(1)}, bf16[128,16,256]{2,1,0:T(8,128)(2,1)S(1)}, bf16[128,16,256]{2,1,0:T(8,128)(2,1)S(1)}) fusion(f32[16,256]{1,0:T(8,128)S(1)} %get-tuple-element.112, f32[16,256]{1,0:T(8,128)S(1)} %get-tuple-element.113, bf16[128,16,512]{2,1,0:T(8,128)(2,1)S(1)} %fusion.55, ...), kind=kLoop, calls=%fused_computation.71 | loop fusion | flops 10485760 | bytes 8454144 | tf_op jit(solution)/shard_map/convert.5
  137.9 0.9 convolution_add_fusion
  (67 shorter events, 6.5 us)
Async XLA Ops:
  6.5 39.3 %all-gather.4.cloned.1.call-start = ((), (), s32[]{:S(2)}) async-start(), calls=%async_computation.1 | async-start | bytes 6291456 | tf_op jit(solution)/shard_map/all_gather | solution.py:133
  10.5 0.7 copy-start.7
  10.5 0.7 copy-start.4
  10.5 33.2 %copy-start.5 = (f32[2048]{0:T(1024)S(1)}, f32[2048]{0:T(1024)}, u32[]{:S(2)}) copy-start(f32[2048]{0:T(1024)} %param.12) | copy-start | bytes 24580
  10.5 33.2 %copy-start.6 = (f32[2048]{0:T(1024)S(1)}, f32[2048]{0:T(1024)}, u32[]{:S(2)}) copy-start(f32[2048]{0:T(1024)} %param.13) | copy-start | bytes 24580
  10.5 33.3 %copy-start.3 = (s32[2,2048]{1,0:T(2,128)S(1)}, s32[2,2048]{1,0:T(2,128)}, u32[]{:S(2)}) copy-start(s32[2,2048]{1,0:T(2,128)} %param.14) | copy-start | bytes 49156
  45.9 13.7 %copy-start.8 = (bf16[4096,1,512]{0,2,1:T(8,128)(2,1)S(1)}, bf16[4096,1,512]{0,2,1:T(8,128)(2,1)}, u32[]{:S(2)}) copy-start(bf16[4096,1,512]{0,2,1:T(8,128)(2,1)} %get-tuple-element.230) | copy-start | bytes 12582916 | tf_op jit(solution)/shard_map/while
  65.4 13.7 %copy-start.8 = (bf16[4096,1,512]{0,2,1:T(8,128)(2,1)S(1)}, bf16[4096,1,512]{0,2,1:T(8,128)(2,1)}, u32[]{:S(2)}) copy-start(bf16[4096,1,512]{0,2,1:T(8,128)(2,1)} %get-tuple-element.230) | copy-start | bytes 12582916 | tf_op jit(solution)/shard_map/while
  84.9 5.7 %copy-start.2 = (s32[64]{0:T(128)S(1)}, s32[64]{0:T(128)}, u32[]{:S(2)}) copy-start(s32[64]{0:T(128)} %param.17) | copy-start | bytes 772
  84.9 31.7 %all-to-all-start = ((bf16[8,128,1,512]{3,1,2,0:T(8,128)(2,1)}), bf16[8,128,1,512]{3,1,2,0:T(8,128)(2,1)S(1)}, u32[]{:S(2)}, u32[]{:S(2)}) async-start(bf16[8,128,1,512]{3,1,2,0:T(8,128)(2,1)} %bitcast.16), calls=%async_computation | async-start | bytes 2097152 | tf_op jit(solution)/shard_map/all_to_all | solution.py:105
  123.3 3.0 %copy-start.1 = (bf16[16,128,512]{2,1,0:T(8,128)(2,1)S(1)}, bf16[16,128,512]{2,1,0:T(8,128)(2,1)}, u32[]{:S(2)}) copy-start(bf16[16,128,512]{2,1,0:T(8,128)(2,1)} %gather_fusion.1) | copy-start | bytes 6291460
  130.1 1.7 %copy-start = (bf16[16,128,512]{2,1,0:T(8,128)(2,1)S(1)}, bf16[16,128,512]{2,1,0:T(8,128)(2,1)}, u32[]{:S(2)}) copy-start(bf16[16,128,512]{2,1,0:T(8,128)(2,1)} %gather_fusion.2) | copy-start | bytes 6291460
Sparse Core Ops, SparseCore 0:
  10.7 16.3 all-gather.3

commit v5 on v3

--- a/solution.py
+++ b/solution.py
@@ -145,9 +145,9 @@
     mine = lax.dynamic_slice_in_dim(split_pos, lax.axis_index("beam"), 1, 2).reshape(
         2, probe_count * half_probes
     )
-    row_total = probe_count * half_probes
-    block_rows = math.gcd(row_total, 512)
-    pos_blocks = mine.reshape(2, row_total // block_rows, block_rows).transpose(1, 0, 2)
+    halves = 2 if half_probes % 16 == 0 else 1
+    part_rows = half_probes // halves
+    pos_parts = mine.reshape(2, probe_count, halves, part_rows).transpose(2, 0, 1, 3)
 
     def whole_block(positions):
         real_coef, imag_coef = coefficients(full_k, full_cos, full_sin, positions)
@@ -159,8 +159,13 @@
         )
         return combine(beam_terms).astype(jnp.bfloat16)
 
-    psi_own = lax.map(whole_block, pos_blocks).reshape(probe_count, half_probes, col_dev, width_two)
-    return apply_patches(psi_own, all_patches, patch_col, det_table)
+    energies = []
+    for part in range(halves):
+        psi_part = whole_block(pos_parts[part].reshape(2, probe_count * part_rows)).reshape(
+            probe_count, part_rows, col_dev, width_two
+        )
+        energies.append(apply_patches(psi_part, all_patches, patch_col, det_table))
+    return jnp.concatenate(energies, axis=1)
 
 
 def solution(mesh):

time: 139 us -> 133 us (0.957)
  waiting for transfers between devices: 25.3 us -> 2.39 us
  matrix products: 13.1 us -> 22.2 us
  other arithmetic: 36.6 us -> 42.9 us
  starting transfers between devices: 5.52 us -> 10.4 us
  local copies, waits for them, and re-layouts: 9.82 us -> 6.31 us
    all_to_all x1 -> x2, waiting for transfers between devices: 25.2 us -> 1.68 us  [apply_patches(): lax.all_to_all(psi_own, 'probe', split_axis=0, concat_axis=2, tiled=True)]
    dot_general x2, matrix products: 9.06 us -> 16.3 us  [whole_block(): jnp.einsum('kpb,bcx->kpcx', jnp.stack([real_coef, imag_coef]), full_matri...]
    all_to_all x1 -> x2, starting transfers between devices: 5.48 us -> 10.4 us  [apply_patches(): lax.all_to_all(psi_own, 'probe', split_axis=0, concat_axis=2, tiled=True)]
    unnamed x19 -> x4, local copies, waits for them, and re-layouts: 4.68 us -> 0.04 us
    gather x4 -> x8, local copies, waits for them, and re-layouts: 2.73 us -> 4.91 us  [add_block(): picked = jnp.take(psi, col_ids, axis=1)]
    dynamic_update_slice x4 -> x0, local copies, waits for them, and re-layouts: 2.11 us -> none  [shards(): lax.map(whole_block, pos_blocks)]
    concatenate x2, other arithmetic: 0.07 us -> 1.71 us  [combine(): jnp.concatenate([beam_terms[0, ..., :half_width] - beam_terms[1, ..., hal...]
    convert_element_type x2 -> x1, other arithmetic: 27.3 us -> 28.5 us  [coefficients(): (beam_cos[None, :] * cos_t - beam_sin[None, :] * sin_t).astype(jnp.bfloat16)]
  transfers between devices with their start and end apart: 2 -> 3, of which waited for: 1 -> 2; matrix products, arithmetic and copies ran while one was open for 1% -> 39% of each run, Pallas kernels for 0% -> 0%
where the time goes in v5:
time: 133 us
  other arithmetic  42.9 us (32%)
  blocking collectives  34.2 us (26%)
  matrix products  22.2 us (17%)
  between operations  13.5 us (10%)
  starting transfers between devices  10.4 us (8%)
  local copies, waits for them, and re-layouts  6.31 us (5%)
  waiting for transfers between devices  2.39 us (2%)
    all_gather x1, blocking collectives, shards(): gathered = lax.all_gather(packed, 'probe', axis=0)  32.2 us
    convert_element_type x1, other arithmetic, coefficients(): (beam_cos[None, :] * cos_t - beam_sin[None, :] * sin_t).astype(jnp.bfloat16)  28.5 us
    dot_general x2, matrix products, whole_block(): jnp.einsum('kpb,bcx->kpcx', jnp.stack([real_coef, imag_coef]), full_matri...  16.3 us
    all_to_all x2, starting transfers between devices, apply_patches(): lax.all_to_all(psi_own, 'probe', split_axis=0, concat_axis=2, tiled=True)  10.4 us
    select_n x16, other arithmetic, add_block(): picked = jnp.take(psi, col_ids, axis=1)  5.19 us
    gather x8, local copies, waits for them, and re-layouts, add_block(): picked = jnp.take(psi, col_ids, axis=1)  4.91 us
    dot_general x8, matrix products, patch_energy(): jnp.einsum('rjx,xq->rjq', wave_out, det_table, preferred_element_type=jnp...  4.01 us
    another operation x11, other arithmetic  3.41 us
  transfers between devices with their start and end apart: 3, of which 2 were waited for; matrix products, arithmetic and copies ran while one was open for 39% of the time, Pallas kernels for 0%

profile of v5, /device:TPU:0, one launch (start us, length us, event | category | flops | bytes accessed | tf_op | source)
XLA Modules:
  0.0 132.5 jit_solution(16797439904189478224)
XLA Ops:
  6.5 0.7 all-gather.4.cloned.1.call-update
  7.3 0.8 slice_convert_fusion.8
  8.1 0.8 cosine_multiply_fusion
  8.9 2.0 %all_gather.12 = f32[4,4096]{1,0:T(4,128)S(1)} all-gather(f32[4,2048]{1,0:T(4,128)S(1)} %pad_maximum_fusion.2), channel_id=1, replica_groups=mesh['grp'=2,'probe'=8,'beam'=2] {'beam'}, dimensions={1}, use_global_device_ids=true | all-gather | bytes 98304 | tf_op jit(solution)/shard_map/all_gather | solution.py:139
  11.0 0.7 convert_bitcast_fusion
  11.7 0.7 convert_bitcast_fusion.1
  12.4 32.2 %all-gather.1 = f32[8,1,4608]{2,1,0:T(1,128)S(1)} all-gather(f32[1,1,4608]{2,1,0:T(1,128)S(1)} %reshape.1177), channel_id=2, replica_groups=mesh['grp'=2,'probe'=8,'beam'=2] {'probe'}, dimensions={0}, use_global_device_ids=true | all-gather | bytes 165888 | tf_op jit(solution)/shard_map/all_gather | solution.py:114
  45.2 0.7 reshape.1151
  46.0 0.6 negate_convert_fusion.2
  46.6 28.5 %subtract_convert_fusion.1 = (bf16[1,512,4096]{2,1,0:T(8,128)(2,1)}, bf16[1,512,4096]{2,1,0:T(8,128)(2,1)}, bf16[1,512,4096]{2,1,0:T(8,128)(2,1)}, bf16[1,512,4096]{2,1,0:T(8,128)(2,1)}) fusion(f32[4096]{0:T(1024)S(1)} %bitcast.104, f32[4096]{0:T(1024)S(1)} %bitcast.103, s32[4096]{0:T(1024)S(1)} %bitcast.106, s32[512]{0:T(512)S(1)} %mul.703, ...), kind=kLoop, calls=%fused_computation.121 | loop fusion | flops 209715200 | bytes 16850944 | tf_op jit(solution)/shard_map/convert_element_type | solution.py:29
  75.1 8.1 %fusion.71 = f32[2,512,1,512]{3,1,0,2:T(8,128)S(1)} fusion(bf16[4096,1,512]{2,0,1:T(8,128)(2,1)} %all-gather.4.cloned.1.call-done, bf16[1,512,4096]{2,1,0:T(8,128)(2,1)} %get-tuple-element.173, bf16[1,512,4096]{2,1,0:T(8,128)(2,1)} %get-tuple-element.172), kind=kOutput, calls=%fused_computation.131 | convolution fusion | flops 4299161600 | bytes 14680064 | tf_op jit(solution)/shard_map/kpb,bcx->kpcx/dot_general | solution.py:154
  83.4 0.9 pad_maximum_fusion
  84.2 5.6 %all-to-all-start = ((bf16[8,64,1,512]{3,1,2,0:T(8,128)(2,1)}), bf16[8,64,1,512]{3,1,2,0:T(8,128)(2,1)S(1)}, u32[]{:S(2)}, u32[]{:S(2)}) async-start(bf16[8,64,1,512]{3,1,2,0:T(8,128)(2,1)} %pad_maximum_fusion), calls=%async_computation | async-start | bytes 1048576 | tf_op jit(solution)/shard_map/all_to_all | solution.py:102
  89.8 8.1 %fusion.66 = f32[2,512,1,512]{3,1,0,2:T(8,128)S(1)} fusion(bf16[4096,1,512]{2,0,1:T(8,128)(2,1)} %all-gather.4.cloned.1.call-done, bf16[1,512,4096]{2,1,0:T(8,128)(2,1)} %get-tuple-element.176, bf16[1,512,4096]{2,1,0:T(8,128)(2,1)} %get-tuple-element.177), kind=kOutput, calls=%fused_computation.130 | convolution fusion | flops 4299161600 | bytes 14680064 | tf_op jit(solution)/shard_map/kpb,bcx->kpcx/dot_general | solution.py:154
  98.1 0.8 pad_maximum_fusion.1
  98.9 1.2 all-to-all-done
  100.1 4.8 %all-to-all-start.1 = ((bf16[8,64,1,512]{3,1,2,0:T(8,128)(2,1)}), bf16[8,64,1,512]{3,1,2,0:T(8,128)(2,1)S(1)}, u32[]{:S(2)}, u32[]{:S(2)}) async-start(bf16[8,64,1,512]{3,1,2,0:T(8,128)(2,1)} %pad_maximum_fusion.1), calls=%async_computation.1 | async-start | bytes 1048576 | tf_op jit(solution)/shard_map/all_to_all | solution.py:102
  104.9 9.8 %while.22 = (s32[]{:T(128)}, f32[8,64]{1,0:T(8,128)S(1)}, s32[4,16]{1,0:T(4,128)S(1)}, bf16[64,8,512]{2,0,1:T(8,128)(2,1)S(1)}, bf16[4,16,512]{2,1,0:T(8,128)(2,...) while((s32[]{:T(128)}, f32[8,64]{1,0:T(8,128)S(1)}, s32[4,16]{1,0:T(4,128)S(1)}, ...), condition=%wide.region_2.4_spmd.clone, body=%wide.region_0.3_spmd.clone.sunk | while | flops 274311584 | bytes 7733831 | solution.py:95
  105.6 0.6 fusion.111
  108.0 0.6 fusion.111
  112.9 0.6 fusion.111
  115.2 9.8 %while.23 = (s32[]{:T(128)}, f32[8,64]{1,0:T(8,128)S(1)}, s32[4,16]{1,0:T(4,128)S(1)}, bf16[64,8,512]{2,0,1:T(8,128)(2,1)S(1)}, bf16[4,16,512]{2,1,0:T(8,128)(2,...) while((s32[]{:T(128)}, f32[8,64]{1,0:T(8,128)S(1)}, s32[4,16]{1,0:T(4,128)S(1)}, ...), condition=%wide.region_5.7_spmd.clone, body=%wide.region_3.6_spmd.clone.sunk | while | flops 274311584 | bytes 7733831 | solution.py:95
  115.9 0.6 fusion.118
  125.0 0.7 pad_maximum_fusion.4
  (105 shorter events, 17.8 us)
Async XLA Ops:
  6.5 68.6 %all-gather.4.cloned.1.call-start = ((), (), s32[]{:S(2)}) async-start(), calls=%async_computation.2 | async-start | bytes 6291456 | tf_op jit(solution)/shard_map/all_gather | solution.py:130
  84.2 15.8 %all-to-all-start = ((bf16[8,64,1,512]{3,1,2,0:T(8,128)(2,1)}), bf16[8,64,1,512]{3,1,2,0:T(8,128)(2,1)S(1)}, u32[]{:S(2)}, u32[]{:S(2)}) async-start(bf16[8,64,1,512]{3,1,2,0:T(8,128)(2,1)} %pad_maximum_fusion), calls=%async_computation | async-start | bytes 1048576 | tf_op jit(solution)/shard_map/all_to_all | solution.py:102
  100.1 15.1 %all-to-all-start.1 = ((bf16[8,64,1,512]{3,1,2,0:T(8,128)(2,1)}), bf16[8,64,1,512]{3,1,2,0:T(8,128)(2,1)S(1)}, u32[]{:S(2)}, u32[]{:S(2)}) async-start(bf16[8,64,1,512]{3,1,2,0:T(8,128)(2,1)} %pad_maximum_fusion.1), calls=%async_computation.1 | async-start | bytes 1048576 | tf_op jit(solution)/shard_map/all_to_all | solution.py:102
Sparse Core Ops, SparseCore 0:
  8.9 16.3 all-gather.3

commit v6 on v5

--- a/solution.py
+++ b/solution.py
@@ -145,7 +145,7 @@
     mine = lax.dynamic_slice_in_dim(split_pos, lax.axis_index("beam"), 1, 2).reshape(
         2, probe_count * half_probes
     )
-    halves = 2 if half_probes % 16 == 0 else 1
+    halves = 4 if half_probes % 32 == 0 else 1
     part_rows = half_probes // halves
     pos_parts = mine.reshape(2, probe_count, halves, part_rows).transpose(2, 0, 1, 3)
 

time: 133 us -> 157 us (1.18)
  starting transfers between devices: 10.4 us -> 21.6 us
  local copies, waits for them, and re-layouts: 6.31 us -> 11.2 us
  matrix products: 22.2 us -> 26.2 us
  other arithmetic: 42.9 us -> 44.5 us
    all_to_all x2 -> x4, starting transfers between devices: 10.4 us -> 21.6 us  [apply_patches(): lax.all_to_all(psi_own, 'probe', split_axis=0, concat_axis=2, tiled=True)]
    gather x8 -> x16, local copies, waits for them, and re-layouts: 4.91 us -> 9.29 us  [add_block(): picked = jnp.take(psi, col_ids, axis=1)]
    dot_general x8 -> x16, matrix products: 1.9 us -> 3.95 us  [add_block(): jnp.einsum('rj,jc->cr', energy, onehot, precision=lax.Precision.HIGHEST)]
    dot_general x8 -> x16, matrix products: 4.01 us -> 5.87 us  [patch_energy(): jnp.einsum('rjx,xq->rjq', wave_out, det_table, preferred_element_type=jnp...]
    another operation x11 -> x21, other arithmetic: 3.41 us -> 3.82 us
    dot_general x2 -> x4, matrix products: 16.3 us -> 16.4 us  [whole_block(): jnp.einsum('kpb,bcx->kpcx', jnp.stack([real_coef, imag_coef]), full_matri...]
    select_n x16 -> x32, other arithmetic: 5.19 us -> 5.26 us  [add_block(): picked = jnp.take(psi, col_ids, axis=1)]
  transfers between devices with their start and end apart: 3 -> 5, of which waited for: 2 -> 3; matrix products, arithmetic and copies ran while one was open for 39% -> 43% of each run, Pallas kernels for 0% -> 0%
where the time goes in v6:
time: 157 us; the launch traced here: 156 us
  other arithmetic  44.5 us (28%)
  blocking collectives  34.2 us (22%)
  matrix products  26.2 us (17%)
  starting transfers between devices  21.6 us (14%)
  between operations  13.6 us (9%)
  local copies, waits for them, and re-layouts  11.2 us (7%)
  waiting for transfers between devices  3.69 us (2%)
    all_gather x1, blocking collectives, shards(): gathered = lax.all_gather(packed, 'probe', axis=0)  32.2 us
    convert_element_type x1, other arithmetic, coefficients(): (beam_cos[None, :] * cos_t - beam_sin[None, :] * sin_t).astype(jnp.bfloat16)  28.2 us
    all_to_all x4, starting transfers between devices, apply_patches(): lax.all_to_all(psi_own, 'probe', split_axis=0, concat_axis=2, tiled=True)  21.6 us
    dot_general x4, matrix products, whole_block(): jnp.einsum('kpb,bcx->kpcx', jnp.stack([real_coef, imag_coef]), full_matri...  16.4 us
    gather x16, local copies, waits for them, and re-layouts, add_block(): picked = jnp.take(psi, col_ids, axis=1)  9.29 us
    dot_general x16, matrix products, patch_energy(): jnp.einsum('rjx,xq->rjq', wave_out, det_table, preferred_element_type=jnp...  5.87 us
    select_n x32, other arithmetic, add_block(): picked = jnp.take(psi, col_ids, axis=1)  5.26 us
    dot_general x16, matrix products, add_block(): jnp.einsum('rj,jc->cr', energy, onehot, precision=lax.Precision.HIGHEST)  3.95 us
  transfers between devices with their start and end apart: 5, of which 3 were waited for; matrix products, arithmetic and copies ran while one was open for 43% of the time, Pallas kernels for 0%

profile of v6, /device:TPU:0, one launch (start us, length us, event | category | flops | bytes accessed | tf_op | source)
XLA Modules:
  0.0 156.0 jit_solution(8879523117622475717)
XLA Ops:
  7.3 0.8 slice_convert_fusion.12
  8.1 0.8 cosine_multiply_fusion
  8.9 2.0 %all_gather.12 = f32[4,4096]{1,0:T(4,128)S(1)} all-gather(f32[4,2048]{1,0:T(4,128)S(1)} %pad_maximum_fusion.4), channel_id=1, replica_groups=mesh['grp'=2,'probe'=8,'beam'=2] {'beam'}, dimensions={1}, use_global_device_ids=true | all-gather | bytes 98304 | tf_op jit(solution)/shard_map/all_gather | solution.py:139
  12.4 32.2 %all-gather.1 = f32[8,1,4608]{2,1,0:T(1,128)S(1)} all-gather(f32[1,1,4608]{2,1,0:T(1,128)S(1)} %reshape.2273), channel_id=2, replica_groups=mesh['grp'=2,'probe'=8,'beam'=2] {'probe'}, dimensions={0}, use_global_device_ids=true | all-gather | bytes 165888 | tf_op jit(solution)/shard_map/all_gather | solution.py:114
  45.6 0.7 reshape.2229
  47.0 28.2 %subtract_convert_fusion.3 = (bf16[1,256,4096]{2,1,0:T(8,128)(2,1)}, bf16[1,256,4096]{2,1,0:T(8,128)(2,1)}, bf16[1,256,4096]{2,1,0:T(8,128)(2,1)}, bf16[1,256,40...) fusion(f32[4096]{0:T(1024)S(1)} %bitcast.176, ...), kind=kLoop, calls=%fused_computation.253 | loop fusion | flops 209715200 | bytes 16850944 | tf_op jit(solution)/shard_map/convert_element_type | solution.py:29
  75.3 5.8 %fusion.147 = f32[2,256,1,512]{3,1,0,2:T(8,128)S(1)} fusion(bf16[4096,1,512]{2,0,1:T(8,128)(2,1)} %all-gather.4.cloned.1.call-done, bf16[1,256,4096]{2,1,0:T(8,128)(2,1)} %get-tuple-element.339, bf16[1,256,4096]{2,1,0:T(8,128)(2,1)} %get-tuple-element.338), kind=kOutput, calls=%fused_computation.263 | convolution fusion | flops 2149580800 | bytes 9437184 | tf_op jit(solution)/shard_map/kpb,bcx->kpcx/dot_general | solution.py:154
  81.1 0.7 pad_maximum_fusion
  81.9 5.6 %all-to-all-start = ((bf16[8,32,1,512]{3,1,2,0:T(8,128)(2,1)}), bf16[8,32,1,512]{3,1,2,0:T(8,128)(2,1)S(1)}, u32[]{:S(2)}, u32[]{:S(2)}) async-start(bf16[8,32,1,512]{3,1,2,0:T(8,128)(2,1)} %pad_maximum_fusion), calls=%async_computation | async-start | bytes 524288 | tf_op jit(solution)/shard_map/all_to_all | solution.py:102
  87.4 5.9 %fusion.142 = f32[2,256,1,512]{3,1,0,2:T(8,128)S(1)} fusion(bf16[4096,1,512]{2,0,1:T(8,128)(2,1)} %all-gather.4.cloned.1.call-done, bf16[1,256,4096]{2,1,0:T(8,128)(2,1)} %get-tuple-element.346, bf16[1,256,4096]{2,1,0:T(8,128)(2,1)} %get-tuple-element.347), kind=kOutput, calls=%fused_computation.262 | convolution fusion | flops 2149580800 | bytes 9437184 | tf_op jit(solution)/shard_map/kpb,bcx->kpcx/dot_general | solution.py:154
  93.5 2.3 %fusion.137 = f32[2,256,1,512]{3,1,0,2:T(8,128)S(1)} fusion(bf16[4096,1,512]{2,0,1:T(8,128)(2,1)S(1)} %copy-done.3, bf16[1,256,4096]{2,1,0:T(8,128)(2,1)S(1)} %copy-done.1, bf16[1,256,4096]{2,1,0:T(8,128)(2,1)S(1)} %copy-done.2), kind=kOutput, calls=%fused_computation.261 | convolution fusion | flops 2149580800 | bytes 9437184 | tf_op jit(solution)/shard_map/kpb,bcx->kpcx/dot_general | solution.py:154
  95.8 0.7 pad_maximum_fusion.1
  96.6 2.3 %fusion.132 = f32[2,256,1,512]{3,1,0,2:T(8,128)S(1)} fusion(bf16[4096,1,512]{2,0,1:T(8,128)(2,1)S(1)} %copy-done.3, bf16[1,256,4096]{2,1,0:T(8,128)(2,1)S(1)} %get-tuple-element.350, bf16[1,256,4096]{2,1,0:T(8,128)(2,1)S(1)} %copy-done), kind=kOutput, calls=%fused_computation.260 | convolution fusion | flops 2149580800 | bytes 9437184 | tf_op jit(solution)/shard_map/kpb,bcx->kpcx/dot_general | solution.py:154
  98.9 0.7 pad_maximum_fusion.2
  100.4 6.0 %all-to-all-start.1 = ((bf16[8,32,1,512]{3,1,2,0:T(8,128)(2,1)}), bf16[8,32,1,512]{3,1,2,0:T(8,128)(2,1)S(1)}, u32[]{:S(2)}, u32[]{:S(2)}) async-start(bf16[8,32,1,512]{3,1,2,0:T(8,128)(2,1)} %pad_maximum_fusion.1), calls=%async_computation.1 | async-start | bytes 524288 | tf_op jit(solution)/shard_map/all_to_all | solution.py:102
  106.4 7.3 %while.44 = (s32[]{:T(128)}, f32[8,32]{1,0:T(8,128)S(1)}, s32[4,16]{1,0:T(4,128)S(1)}, bf16[32,8,512]{2,0,1:T(8,128)(2,1)S(1)}, bf16[4,16,512]{2,1,0:T(8,128)(2,...) while((s32[]{:T(128)}, f32[8,32]{1,0:T(8,128)S(1)}, s32[4,16]{1,0:T(4,128)S(1)}, ...), condition=%wide.region_2.4_spmd.clone, body=%wide.region_0.3_spmd.clone.sunk | while | flops 137160592 | bytes 4057671 | solution.py:95
  113.7 1.0 all-to-all-done.1
  114.6 5.1 %all-to-all-start.2 = ((bf16[8,32,1,512]{3,1,2,0:T(8,128)(2,1)}), bf16[8,32,1,512]{3,1,2,0:T(8,128)(2,1)S(1)}, u32[]{:S(2)}, u32[]{:S(2)}) async-start(bf16[8,32,1,512]{3,1,2,0:T(8,128)(2,1)} %pad_maximum_fusion.2), calls=%async_computation.2 | async-start | bytes 524288 | tf_op jit(solution)/shard_map/all_to_all | solution.py:102
  119.7 7.3 %while.45 = (s32[]{:T(128)}, f32[8,32]{1,0:T(8,128)S(1)}, s32[4,16]{1,0:T(4,128)S(1)}, bf16[32,8,512]{2,0,1:T(8,128)(2,1)S(1)}, bf16[4,16,512]{2,1,0:T(8,128)(2,...) while((s32[]{:T(128)}, f32[8,32]{1,0:T(8,128)S(1)}, s32[4,16]{1,0:T(4,128)S(1)}, ...), condition=%wide.region_5.7_spmd.clone, body=%wide.region_3.6_spmd.clone.sunk | while | flops 137160592 | bytes 4057671 | solution.py:95
  127.0 1.1 all-to-all-done.2
  128.0 5.0 %all-to-all-start.3 = ((bf16[8,32,1,512]{3,1,2,0:T(8,128)(2,1)}), bf16[8,32,1,512]{3,1,2,0:T(8,128)(2,1)S(1)}, u32[]{:S(2)}, u32[]{:S(2)}) async-start(bf16[8,32,1,512]{3,1,2,0:T(8,128)(2,1)} %pad_maximum_fusion.3), calls=%async_computation.3 | async-start | bytes 524288 | tf_op jit(solution)/shard_map/all_to_all | solution.py:102
  133.0 7.3 %while.46 = (s32[]{:T(128)}, f32[8,32]{1,0:T(8,128)S(1)}, s32[4,16]{1,0:T(4,128)S(1)}, bf16[32,8,512]{2,0,1:T(8,128)(2,1)S(1)}, bf16[4,16,512]{2,1,0:T(8,128)(2,...) while((s32[]{:T(128)}, f32[8,32]{1,0:T(8,128)S(1)}, s32[4,16]{1,0:T(4,128)S(1)}, ...), condition=%wide.region_8.10_spmd.clone, body=%wide.region_6.9_spmd.clone.sunk | while | flops 137160592 | bytes 4057671 | solution.py:95
  140.2 1.0 all-to-all-done.3
  141.2 7.3 %while.47 = (s32[]{:T(128)}, f32[8,32]{1,0:T(8,128)S(1)}, s32[4,16]{1,0:T(4,128)S(1)}, bf16[32,8,512]{2,0,1:T(8,128)(2,1)S(1)}, bf16[4,16,512]{2,1,0:T(8,128)(2,...) while((s32[]{:T(128)}, f32[8,32]{1,0:T(8,128)S(1)}, s32[4,16]{1,0:T(4,128)S(1)}, ...), condition=%wide.region_11.13_spmd.clone, body=%wide.region_9.12_spmd.clone.sunk | while | flops 137160592 | bytes 4057671 | solution.py:95
  (211 shorter events, 33.4 us)
Async XLA Ops:
  6.5 68.7 %all-gather.4.cloned.1.call-start = ((), (), s32[]{:S(2)}) async-start(), calls=%async_computation.4 | async-start | bytes 6291456 | tf_op jit(solution)/shard_map/all_gather | solution.py:130
  81.9 18.6 %all-to-all-start = ((bf16[8,32,1,512]{3,1,2,0:T(8,128)(2,1)}), bf16[8,32,1,512]{3,1,2,0:T(8,128)(2,1)S(1)}, u32[]{:S(2)}, u32[]{:S(2)}) async-start(bf16[8,32,1,512]{3,1,2,0:T(8,128)(2,1)} %pad_maximum_fusion), calls=%async_computation | async-start | bytes 524288 | tf_op jit(solution)/shard_map/all_to_all | solution.py:102
  87.4 6.0 %copy-start.1 = (bf16[1,256,4096]{2,1,0:T(8,128)(2,1)S(1)}, bf16[1,256,4096]{2,1,0:T(8,128)(2,1)}, u32[]{:S(2)}) copy-start(bf16[1,256,4096]{2,1,0:T(8,128)(2,1)} %get-tuple-element.348) | copy-start | bytes 6291460
  87.4 6.0 %copy-start.2 = (bf16[1,256,4096]{2,1,0:T(8,128)(2,1)S(1)}, bf16[1,256,4096]{2,1,0:T(8,128)(2,1)}, u32[]{:S(2)}) copy-start(bf16[1,256,4096]{2,1,0:T(8,128)(2,1)} %get-tuple-element.349) | copy-start | bytes 6291460
  87.4 6.0 %copy-start.3 = (bf16[4096,1,512]{2,0,1:T(8,128)(2,1)S(1)}, bf16[4096,1,512]{2,0,1:T(8,128)(2,1)}, u32[]{:S(2)}) copy-start(bf16[4096,1,512]{2,0,1:T(8,128)(2,1)} %all-gather.4.cloned.1.call-done) | copy-start | bytes 12582916
  93.5 3.1 %copy-start = (bf16[1,256,4096]{2,1,0:T(8,128)(2,1)S(1)}, bf16[1,256,4096]{2,1,0:T(8,128)(2,1)}, u32[]{:S(2)}) copy-start(bf16[1,256,4096]{2,1,0:T(8,128)(2,1)} %get-tuple-element.351) | copy-start | bytes 6291460
  100.4 14.2 %all-to-all-start.1 = ((bf16[8,32,1,512]{3,1,2,0:T(8,128)(2,1)}), bf16[8,32,1,512]{3,1,2,0:T(8,128)(2,1)S(1)}, u32[]{:S(2)}, u32[]{:S(2)}) async-start(bf16[8,32,1,512]{3,1,2,0:T(8,128)(2,1)} %pad_maximum_fusion.1), calls=%async_computation.1 | async-start | bytes 524288 | tf_op jit(solution)/shard_map/all_to_all | solution.py:102
  114.6 13.4 %all-to-all-start.2 = ((bf16[8,32,1,512]{3,1,2,0:T(8,128)(2,1)}), bf16[8,32,1,512]{3,1,2,0:T(8,128)(2,1)S(1)}, u32[]{:S(2)}, u32[]{:S(2)}) async-start(bf16[8,32,1,512]{3,1,2,0:T(8,128)(2,1)} %pad_maximum_fusion.2), calls=%async_computation.2 | async-start | bytes 524288 | tf_op jit(solution)/shard_map/all_to_all | solution.py:102
  128.0 13.2 %all-to-all-start.3 = ((bf16[8,32,1,512]{3,1,2,0:T(8,128)(2,1)}), bf16[8,32,1,512]{3,1,2,0:T(8,128)(2,1)S(1)}, u32[]{:S(2)}, u32[]{:S(2)}) async-start(bf16[8,32,1,512]{3,1,2,0:T(8,128)(2,1)} %pad_maximum_fusion.3), calls=%async_computation.3 | async-start | bytes 524288 | tf_op jit(solution)/shard_map/all_to_all | solution.py:102
Sparse Core Ops, SparseCore 0:
  8.9 16.3 all-gather.3
